TPU v7x, 128 devices: a whole 4x4x4 slice. The times are simulated.
128 devices in a mesh: gx: 8 (over y, core), gy: 4 (over z), gz: 4 (over x).
Axes of the slice: x: 4, y: 4, z: 4, core: 2. Of those that a mesh axis runs over, the one named last changes fastest.
Arguments:
- velocity: float32 [3, 64, 128, 512], P(None, 'gx', 'gz', 'gy'), may hold values from -4 to 4
- pressure: float32 [64, 128, 512], P('gx', 'gz', 'gy'), may hold values from -4 to 4
- viscosity: float32 [64, 128, 512], P('gx', 'gz', 'gy'), may hold values from 0.1 to 10
- body_force: float32 [3, 64, 128, 512], P(None, 'gx', 'gz', 'gy'), may hold values from -6 to 6
Outputs:
- velocity_out: float32 [3, 64, 128, 512], P(None, 'gx', 'gz', 'gy')
- pressure_out: float32 [64, 128, 512], P('gx', 'gz', 'gy')
All inputs are finite; a program needn't handle non-finite values.
Results may differ from a plain program's by a relative error of at most 0.00002.
Values sent between devices are 32-bit elements; how exact they have to be, the bound alone decides.
A program may use at most 128 MiB of HBM per device.

v0:
```python
import jax
import jax.numpy as jnp
from jax import lax
from jax.sharding import PartitionSpec as P

COARSE = 4
POST = 2


relax_weight = 0.6
uzawa_step = 0.5


def padded_2(array, sides, width):
    for axis, dim in sides:
        count, length = (lax.axis_size(axis), array.shape[dim])
        up = [(i, (i + 1) % count) for i in range(count - 1)]
        down = [(j, i) for i, j in up]
        last = lax.slice_in_dim(array, length - width, length, axis=dim)
        first = lax.slice_in_dim(array, 0, width, axis=dim)
        before = lax.ppermute(last, axis, up)
        after = lax.ppermute(first, axis, down)
        array = jnp.concatenate([before, array, after], axis=dim)
    return array


def extended(array, sides, width):
    edges = {}
    for axis, dim in sides:
        count, length = (lax.axis_size(axis), array.shape[dim])
        up = [(i, (i + 1) % count) for i in range(count - 1)]
        last = lax.slice_in_dim(array, length - width, length, axis=dim)
        first = lax.slice_in_dim(array, 0, width, axis=dim)
        edges[dim] = (
            lax.ppermute(last, axis, up),
            lax.ppermute(first, axis, [(b, a) for a, b in up]),
        )
    done = []
    for _, dim in sides:
        low, high = edges[dim]
        around = [(width, width) if d in done else (0, 0) for d in range(array.ndim)]
        array = jnp.concatenate([jnp.pad(low, around), array, jnp.pad(high, around)], axis=dim)
        done.append(dim)
    return array


def window(padded, spatial, offset):
    leading = padded.ndim - 3
    selection = [slice(None)] * leading
    for axis_id in range(3):
        extent = padded.shape[leading + axis_id]
        if axis_id == spatial:
            selection.append(slice(1 + offset, extent - 1 + offset))
        else:
            selection.append(slice(1, extent - 1))
    return padded[tuple(selection)]


def operator_terms(padded_fields, padded_visc, right_side, source, spacing):
    visc_cell = window(padded_visc, 0, 0)
    velocity = window(padded_fields[:3], 0, 0)
    inverse_sq = 1.0 / (spacing * spacing)
    half_inverse = 0.5 / spacing
    diagonal = jnp.zeros_like(visc_cell)
    viscous = jnp.zeros_like(velocity)
    divergence = jnp.zeros_like(visc_cell)
    gradients = []
    for spatial in range(3):
        for offset in (1, -1):
            face_visc = 0.5 * (visc_cell + window(padded_visc, spatial, offset))
            diagonal = diagonal + face_visc
            viscous = viscous + face_visc * (velocity - window(padded_fields[:3], spatial, offset))
        gradients.append(
            (window(padded_fields[3], spatial, 1) - window(padded_fields[3], spatial, -1))
            * half_inverse
        )
        divergence = (
            divergence
            + (
                window(padded_fields[spatial], spatial, 1)
                - window(padded_fields[spatial], spatial, -1)
            )
            * half_inverse
        )
    momentum = right_side - viscous * inverse_sq - jnp.stack(gradients)
    continuity = source - divergence
    return (momentum, continuity, diagonal * inverse_sq, visc_cell)


def relax_sweep(padded_fields, padded_visc, right_side, source, spacing):
    momentum, continuity, diagonal, visc_cell = operator_terms(
        padded_fields, padded_visc, right_side, source, spacing
    )
    velocity = window(padded_fields[:3], 0, 0)
    pressure = window(padded_fields[3], 0, 0)
    new_velocity = velocity + relax_weight * momentum / diagonal
    new_pressure = pressure + uzawa_step * visc_cell * continuity
    return jnp.concatenate([new_velocity, new_pressure[None]], axis=0)


def restrict(stacked):
    extents = stacked.shape
    blocks = stacked.reshape(extents[0], extents[1] // 2, 2, extents[2] // 2, 2, extents[3] // 2, 2)
    return blocks.mean(axis=(2, 4, 6))


def prolong(coarse_fields):
    return jnp.repeat(jnp.repeat(jnp.repeat(coarse_fields, 2, axis=1), 2, axis=2), 2, axis=3)


def fine_rim(fields):
    return padded_2(fields, (("gx", 1), ("gy", 3), ("gz", 2)), 1)


def zero_padded(coarse):
    return jnp.zeros(
        (4, coarse.shape[1] + 2, coarse.shape[2] + 2, coarse.shape[3] + 2), jnp.float32
    )


def local(velocity, pressure, viscosity, body_force):
    fields = jnp.concatenate([velocity, pressure[None]], axis=0)
    stacked = jnp.concatenate([fields, viscosity[None]], axis=0)
    deep = extended(stacked, (("gx", 1), ("gy", 3), ("gz", 2)), 2)
    padded_visc = deep[4, 1:-1, 1:-1, 1:-1]
    deep_coarse = restrict(deep[4:5])[0]
    fields = relax_sweep(deep[:4, 1:-1, 1:-1, 1:-1], padded_visc, body_force, 0.0, 1.0)
    fields = relax_sweep(fine_rim(fields), padded_visc, body_force, 0.0, 1.0)
    momentum, continuity, diagonal, visc_cell = operator_terms(
        fine_rim(fields), padded_visc, body_force, 0.0, 1.0
    )
    packed = restrict(jnp.concatenate([momentum, continuity[None], viscosity[None]], axis=0))
    correction = relax_sweep(zero_padded(packed), deep_coarse, packed[:3], packed[3], 2.0)
    for repeat_index in range(COARSE - 1):
        correction = relax_sweep(
            extended(correction, (("gx", 1), ("gy", 3), ("gz", 2)), 1),
            deep_coarse,
            packed[:3],
            packed[3],
            2.0,
        )
    fields = fields + prolong(correction)
    for repeat_index in range(POST):
        fields = relax_sweep(fine_rim(fields), padded_visc, body_force, 0.0, 1.0)
    return (fields[:3], fields[3])


def solution(mesh):
    return jax.shard_map(
        local,
        mesh=mesh,
        in_specs=(
            P(None, "gx", "gz", "gy"),
            P("gx", "gz", "gy"),
            P("gx", "gz", "gy"),
            P(None, "gx", "gz", "gy"),
        ),
        out_specs=(P(None, "gx", "gz", "gy"), P("gx", "gz", "gy")),
        check_vma=False,
    )
```

profile of v0, /device:TPU:1, one launch (start us, length us, event | category | flops | bytes accessed | tf_op | source)
XLA Modules:
  0.0 318.5 jit_solution(10120477487648530027)
XLA Ops:
  3.0 4.6 %collective-permute-start = (f32[5,8,2,128]{3,1,2,0:T(8,128)S(1)}, f32[5,8,2,128]{3,1,2,0:T(8,128)S(1)}, u32[]{:S(2)}, u32[]{:S(2)}) collective-permute-start(f32[5,8,2,128]{3,1,2,0:T(8,128)S(1)} %copy.591), channel_id=1, source_target_pairs={{0,1},{1,2},{2,3},{4,5},{5,6},{6,7},{8,9},{9,10},{10,11},{12,13},{... | collective-permute-start | bytes 122888 | tf_op jit(solution)/shard_map/ppermute | solution.py:35
  8.8 4.6 %collective-permute-start.2 = (f32[5,2,32,128]{3,2,1,0:T(8,128)S(1)}, f32[5,2,32,128]{3,2,1,0:T(8,128)S(1)}, u32[]{:S(2)}, u32[]{:S(2)}) collective-permute-start(f32[5,2,32,128]{3,2,1,0:T(8,128)S(1)} %get-tuple-element.69), channel_id=1, source_target_pairs={{0,16},{16,32},{32,48},{48,64},{64,80},{80,96},{96,112},{1,17},{17... | collective-permute-start | bytes 491528 | tf_op jit(solution)/shard_map/ppermute | solution.py:35
  13.4 1.9 collective-permute-start.3
  15.8 3.5 %collective-permute-start.1 = (f32[5,8,32,2]{2,1,3,0:T(8,128)S(1)}, f32[5,8,32,2]{2,1,3,0:T(8,128)S(1)}, u32[]{:S(2)}, u32[]{:S(2)}) collective-permute-start(f32[5,8,32,2]{2,1,3,0:T(8,128)S(1)} %copy.592), channel_id=1, source_target_pairs={{0,4},{4,8},{8,12},{1,5},{5,9},{9,13},{2,6},{6,10},{10,14},{3,7},{... | collective-permute-start | bytes 30728 | tf_op jit(solution)/shard_map/ppermute | solution.py:35
  22.2 3.3 %collective-permute-done.4 = f32[5,8,32,2]{2,1,3,0:T(8,128)S(1)} collective-permute-done((f32[5,8,32,2]{2,1,3,0:T(8,128)S(1)}, f32[5,8,32,2]{2,1,3,0:T(8,128)S(1)}, u32[]{:S(2)}, u32[]{:S(2)}) %collective-permute-start.4) | collective-permute-done | bytes 10272 | tf_op jit(solution)/shard_map/ppermute | solution.py:36
  31.8 5.7 %collective-permute-start.7 = (f32[4,1,32,128]{3,2,1,0:T(8,128)S(1)}, f32[4,1,32,128]{3,2,1,0:T(8,128)S(1)}, u32[]{:S(2)}, u32[]{:S(2)}) collective-permute-start(f32[4,1,32,128]{3,2,1,0:T(8,128)S(1)} %get-tuple-element.77), channel_id=1, source_target_pairs={{0,16},{16,32},{32,48},{48,64},{64,80},{80,96},{96,112},{1,17},{17... | collective-permute-start | bytes 196616 | tf_op jit(solution)/shard_map/ppermute | solution.py:21
  39.5 3.6 %collective-permute-done.6 = f32[4,1,32,128]{3,2,1,0:T(8,128)S(1)} collective-permute-done((f32[4,1,32,128]{3,2,1,0:T(8,128)S(1)}, f32[4,1,32,128]{3,2,1,0:T(8,128)S(1)}, u32[]{:S(2)}, u32[]{:S(2)}) %collective-permute-start.6) | collective-permute-done | bytes 65568 | tf_op jit(solution)/shard_map/ppermute | solution.py:22
  47.2 4.3 %collective-permute-start.8 = (f32[4,10,32,1]{2,0,3,1:T(4,128)S(1)}, f32[4,10,32,1]{2,0,3,1:T(4,128)S(1)}, u32[]{:S(2)}, u32[]{:S(2)}) collective-permute-start(f32[4,10,32,1]{2,0,3,1:T(4,128)S(1)} %copy.595), channel_id=1, source_target_pairs={{0,4},{4,8},{8,12},{1,5},{5,9},{9,13},{2,6},{6,10},{10,14},{3,7},{... | collective-permute-start | bytes 15368 | tf_op jit(solution)/shard_map/ppermute | solution.py:21
  53.0 3.1 collective-permute-start.11
  57.5 3.4 %collective-permute-done.10 = f32[4,10,1,130]{3,0,2,1:T(4,128)S(1)} collective-permute-done((f32[4,10,1,130]{3,0,2,1:T(4,128)S(1)}, f32[4,10,1,130]{3,0,2,1:T(4,128)S(1)}, u32[]{:S(2)}, u32[]{:S(2)}) %collective-permute-start.10) | collective-permute-done | bytes 20832 | tf_op jit(solution)/shard_map/ppermute | solution.py:22
  63.8 4.2 %collective-permute-start.13 = (f32[4,1,32,128]{3,2,1,0:T(8,128)S(1)}, f32[4,1,32,128]{3,2,1,0:T(8,128)S(1)}, u32[]{:S(2)}, u32[]{:S(2)}) collective-permute-start(f32[4,1,32,128]{3,2,1,0:T(8,128)S(1)} %get-tuple-element.75), channel_id=1, source_target_pairs={{0,16},{16,32},{32,48},{48,64},{64,80},{80,96},{96,112},{1,17},{17... | collective-permute-start | bytes 196616 | tf_op jit(solution)/shard_map/ppermute | solution.py:21
  69.9 3.6 %collective-permute-done.12 = f32[4,1,32,128]{3,2,1,0:T(8,128)S(1)} collective-permute-done((f32[4,1,32,128]{3,2,1,0:T(8,128)S(1)}, f32[4,1,32,128]{3,2,1,0:T(8,128)S(1)}, u32[]{:S(2)}, u32[]{:S(2)}) %collective-permute-start.12) | collective-permute-done | bytes 65568 | tf_op jit(solution)/shard_map/ppermute | solution.py:22
  76.1 3.9 %collective-permute-start.14 = (f32[4,10,32,1]{2,0,3,1:T(4,128)S(1)}, f32[4,10,32,1]{2,0,3,1:T(4,128)S(1)}, u32[]{:S(2)}, u32[]{:S(2)}) collective-permute-start(f32[4,10,32,1]{2,0,3,1:T(4,128)S(1)} %copy.552), channel_id=1, source_target_pairs={{0,4},{4,8},{8,12},{1,5},{5,9},{9,13},{2,6},{6,10},{10,14},{3,7},{... | collective-permute-start | bytes 15368 | tf_op jit(solution)/shard_map/ppermute | solution.py:21
  81.9 9.7 %concatenate.282 = f32[1,4,2,16,2,64,2]{6,5,4,3,2,1,0:T(8,128)} reshape(f32[8,32,128]{2,1,0:T(8,128)S(1)} %copy-done.19) | data formatting | bytes 262144 | tf_op jit(solution)/shard_map/concatenate | solution.py:132
  91.6 7.5 %reshape.41 = f32[6,2,18,2,66,2]{5,4,3,2,1,0:T(8,128)} reshape(f32[1,12,36,132]{3,2,1,0:T(8,128)S(1)} %slice-done) | data formatting | bytes 456192 | tf_op jit(solution)/shard_map/reshape | solution.py:103
  99.1 7.4 %reduce_sum.19 = f32[6,18,66]{2,1,0:T(8,128)S(1)} reduce(f32[6,2,18,2,66,2]{5,4,3,2,1,0:T(8,128)} %reshape.41, f32[]{:T(128)} %constant.9.clone.1), dimensions={1,3,5}, to_apply=%region_1.2 | reduce | flops 49896 | bytes 256612 | tf_op jit(solution)/shard_map/reduce_sum | solution.py:104
  108.9 4.0 %collective-permute-start.17 = (f32[4,10,1,130]{3,0,2,1:T(4,128)S(1)}, f32[4,10,1,130]{3,0,2,1:T(4,128)S(1)}, u32[]{:S(2)}, u32[]{:S(2)}) collective-permute-start(f32[4,10,1,130]{3,0,2,1:T(4,128)S(1)} %copy.558), channel_id=1, source_target_pairs={{0,1},{1,2},{2,3},{4,5},{5,6},{6,7},{8,9},{9,10},{10,11},{12,13},{... | collective-permute-start | bytes 62408 | tf_op jit(solution)/shard_map/ppermute | solution.py:21
  116.8 10.5 %concatenate.281 = f32[1,4,2,16,2,64,2]{6,5,4,3,2,1,0:T(8,128)} reshape(f32[8,32,128]{2,1,0:T(8,128)} %fusion.152) | data formatting | bytes 262144 | tf_op jit(solution)/shard_map/concatenate | solution.py:132
  127.3 2.5 fusion.73
  129.8 27.3 %concatenate.280 = f32[3,4,2,16,2,64,2]{6,5,4,3,2,1,0:T(8,128)} reshape(f32[3,8,32,128]{3,2,1,0:T(8,128)} %fusion.73) | data formatting | bytes 786432 | tf_op jit(solution)/shard_map/concatenate | solution.py:132
  157.1 14.7 %maximum_reduce_fusion = f32[5,4,16,64]{3,2,1,0:T(8,128)S(1)} fusion(f32[1,4,2,16,2,64,2]{6,5,4,3,2,1,0:T(8,128)} %concatenate.282, f32[1,4,2,16,2,64,2]{6,5,4,3,2,1,0:T(8,128)} %concatenate.281, f32[3,4,2,16,2,64,2]{6,5,4,3,2,1,0:T(8,128)} %concatenate.280), kind=kLoop, calls=%fused_computation | loop fusion | flops 471040 | bytes 737280 | tf_op jit(solution)/shard_map/reduce_sum | solution.py:104
  173.3 4.3 %collective-permute-start.23 = (f32[4,4,1,64]{3,2,1,0:T(1,128)S(1)}, f32[4,4,1,64]{3,2,1,0:T(1,128)S(1)}, u32[]{:S(2)}, u32[]{:S(2)}) collective-permute-start(f32[4,4,1,64]{3,2,1,0:T(1,128)S(1)} %get-tuple-element.123), channel_id=1, source_target_pairs={{0,1},{1,2},{2,3},{4,5},{5,6},{6,7},{8,9},{9,10},{10,11},{12,13},{... | collective-permute-start | bytes 12296 | tf_op jit(solution)/shard_map/ppermute | solution.py:35
  177.6 4.1 %collective-permute-start.19 = (f32[4,1,16,64]{3,2,1,0:T(8,128)S(1)}, f32[4,1,16,64]{3,2,1,0:T(8,128)S(1)}, u32[]{:S(2)}, u32[]{:S(2)}) collective-permute-start(f32[4,1,16,64]{3,2,1,0:T(8,128)S(1)} %get-tuple-element.126), channel_id=1, source_target_pairs={{0,16},{16,32},{32,48},{48,64},{64,80},{80,96},{96,112},{1,17},{17... | collective-permute-start | bytes 49160 | tf_op jit(solution)/shard_map/ppermute | solution.py:35
  185.0 5.3 %collective-permute-done.21 = f32[4,4,16,1]{3,2,1,0:T(8,128)S(1)} collective-permute-done((f32[4,4,16,1]{3,2,1,0:T(8,128)S(1)}, f32[4,4,16,1]{3,2,1,0:T(8,128)S(1)}, u32[]{:S(2)}, u32[]{:S(2)}) %collective-permute-start.21) | collective-permute-done | bytes 1056 | tf_op jit(solution)/shard_map/ppermute | solution.py:36
  190.4 3.7 %collective-permute-start.20 = (f32[4,4,16,1]{3,2,1,0:T(8,128)S(1)}, f32[4,4,16,1]{3,2,1,0:T(8,128)S(1)}, u32[]{:S(2)}, u32[]{:S(2)}) collective-permute-start(f32[4,4,16,1]{3,2,1,0:T(8,128)S(1)} %get-tuple-element.125), channel_id=1, source_target_pairs={{0,4},{4,8},{8,12},{1,5},{5,9},{9,13},{2,6},{6,10},{10,14},{3,7},{... | collective-permute-start | bytes 3080 | tf_op jit(solution)/shard_map/ppermute | solution.py:35
  194.1 2.2 collective-permute-done.20
  198.6 4.0 %collective-permute-start.29 = (f32[4,4,1,64]{3,2,1,0:T(1,128)S(1)}, f32[4,4,1,64]{3,2,1,0:T(1,128)S(1)}, u32[]{:S(2)}, u32[]{:S(2)}) collective-permute-start(f32[4,4,1,64]{3,2,1,0:T(1,128)S(1)} %get-tuple-element.117), channel_id=1, source_target_pairs={{0,1},{1,2},{2,3},{4,5},{5,6},{6,7},{8,9},{9,10},{10,11},{12,13},{... | collective-permute-start | bytes 12296 | tf_op jit(solution)/shard_map/ppermute | solution.py:35
  202.6 6.2 %collective-permute-start.25 = (f32[4,1,16,64]{3,2,1,0:T(8,128)S(1)}, f32[4,1,16,64]{3,2,1,0:T(8,128)S(1)}, u32[]{:S(2)}, u32[]{:S(2)}) collective-permute-start(f32[4,1,16,64]{3,2,1,0:T(8,128)S(1)} %get-tuple-element.120), channel_id=1, source_target_pairs={{0,16},{16,32},{32,48},{48,64},{64,80},{80,96},{96,112},{1,17},{17... | collective-permute-start | bytes 49160 | tf_op jit(solution)/shard_map/ppermute | solution.py:35
  212.2 5.1 %collective-permute-done.27 = f32[4,4,16,1]{3,2,1,0:T(8,128)S(1)} collective-permute-done((f32[4,4,16,1]{3,2,1,0:T(8,128)S(1)}, f32[4,4,16,1]{3,2,1,0:T(8,128)S(1)}, u32[]{:S(2)}, u32[]{:S(2)}) %collective-permute-start.27) | collective-permute-done | bytes 1056 | tf_op jit(solution)/shard_map/ppermute | solution.py:36
  217.3 3.6 %collective-permute-start.26 = (f32[4,4,16,1]{3,2,1,0:T(8,128)S(1)}, f32[4,4,16,1]{3,2,1,0:T(8,128)S(1)}, u32[]{:S(2)}, u32[]{:S(2)}) collective-permute-start(f32[4,4,16,1]{3,2,1,0:T(8,128)S(1)} %get-tuple-element.119), channel_id=1, source_target_pairs={{0,4},{4,8},{8,12},{1,5},{5,9},{9,13},{2,6},{6,10},{10,14},{3,7},{... | collective-permute-start | bytes 3080 | tf_op jit(solution)/shard_map/ppermute | solution.py:35
  223.6 3.6 %collective-permute-start.35 = (f32[4,4,1,64]{3,2,1,0:T(1,128)S(1)}, f32[4,4,1,64]{3,2,1,0:T(1,128)S(1)}, u32[]{:S(2)}, u32[]{:S(2)}) collective-permute-start(f32[4,4,1,64]{3,2,1,0:T(1,128)S(1)} %get-tuple-element.110), channel_id=1, source_target_pairs={{0,1},{1,2},{2,3},{4,5},{5,6},{6,7},{8,9},{9,10},{10,11},{12,13},{... | collective-permute-start | bytes 12296 | tf_op jit(solution)/shard_map/ppermute | solution.py:35
  228.5 5.9 %collective-permute-start.31 = (f32[4,1,16,64]{3,2,1,0:T(8,128)S(1)}, f32[4,1,16,64]{3,2,1,0:T(8,128)S(1)}, u32[]{:S(2)}, u32[]{:S(2)}) collective-permute-start(f32[4,1,16,64]{3,2,1,0:T(8,128)S(1)} %get-tuple-element.114), channel_id=1, source_target_pairs={{0,16},{16,32},{32,48},{48,64},{64,80},{80,96},{96,112},{1,17},{17... | collective-permute-start | bytes 49160 | tf_op jit(solution)/shard_map/ppermute | solution.py:35
  236.5 4.1 %collective-permute-start.32 = (f32[4,4,16,1]{3,2,1,0:T(8,128)S(1)}, f32[4,4,16,1]{3,2,1,0:T(8,128)S(1)}, u32[]{:S(2)}, u32[]{:S(2)}) collective-permute-start(f32[4,4,16,1]{3,2,1,0:T(8,128)S(1)} %get-tuple-element.112), channel_id=1, source_target_pairs={{0,4},{4,8},{8,12},{1,5},{5,9},{9,13},{2,6},{6,10},{10,14},{3,7},{... | collective-permute-start | bytes 3080 | tf_op jit(solution)/shard_map/ppermute | solution.py:35
  240.6 1.9 collective-permute-done.32
  243.8 4.8 %collective-permute-done.33 = f32[4,4,16,1]{3,2,1,0:T(8,128)S(1)} collective-permute-done((f32[4,4,16,1]{3,2,1,0:T(8,128)S(1)}, f32[4,4,16,1]{3,2,1,0:T(8,128)S(1)}, u32[]{:S(2)}, u32[]{:S(2)}) %collective-permute-start.33) | collective-permute-done | bytes 1056 | tf_op jit(solution)/shard_map/ppermute | solution.py:36
  251.7 2.2 copy.566
  253.9 5.7 %collective-permute-start.37 = (f32[4,1,32,128]{3,2,1,0:T(8,128)S(1)}, f32[4,1,32,128]{3,2,1,0:T(8,128)S(1)}, u32[]{:S(2)}, u32[]{:S(2)}) collective-permute-start(f32[4,1,32,128]{3,2,1,0:T(8,128)S(1)} %get-tuple-element.73), channel_id=1, source_target_pairs={{0,16},{16,32},{32,48},{48,64},{64,80},{80,96},{96,112},{1,17},{17... | collective-permute-start | bytes 196616 | tf_op jit(solution)/shard_map/ppermute | solution.py:21
  259.6 1.9 collective-permute-start.36
  261.6 3.6 %collective-permute-done.36 = f32[4,1,32,128]{3,2,1,0:T(8,128)S(1)} collective-permute-done((f32[4,1,32,128]{3,2,1,0:T(8,128)S(1)}, f32[4,1,32,128]{3,2,1,0:T(8,128)S(1)}, u32[]{:S(2)}, u32[]{:S(2)}) %collective-permute-start.36) | collective-permute-done | bytes 65568 | tf_op jit(solution)/shard_map/ppermute | solution.py:22
  269.3 4.3 %collective-permute-start.38 = (f32[4,10,32,1]{2,0,3,1:T(4,128)S(1)}, f32[4,10,32,1]{2,0,3,1:T(4,128)S(1)}, u32[]{:S(2)}, u32[]{:S(2)}) collective-permute-start(f32[4,10,32,1]{2,0,3,1:T(4,128)S(1)} %copy.567), channel_id=1, source_target_pairs={{0,4},{4,8},{8,12},{1,5},{5,9},{9,13},{2,6},{6,10},{10,14},{3,7},{... | collective-permute-start | bytes 15368 | tf_op jit(solution)/shard_map/ppermute | solution.py:21
  275.1 4.3 %collective-permute-start.41 = (f32[4,10,1,130]{3,0,2,1:T(4,128)S(1)}, f32[4,10,1,130]{3,0,2,1:T(4,128)S(1)}, u32[]{:S(2)}, u32[]{:S(2)}) collective-permute-start(f32[4,10,1,130]{3,0,2,1:T(4,128)S(1)} %copy.573), channel_id=1, source_target_pairs={{0,1},{1,2},{2,3},{4,5},{5,6},{6,7},{8,9},{9,10},{10,11},{12,13},{... | collective-permute-start | bytes 62408 | tf_op jit(solution)/shard_map/ppermute | solution.py:21
  280.8 3.4 %collective-permute-done.40 = f32[4,10,1,130]{3,0,2,1:T(4,128)S(1)} collective-permute-done((f32[4,10,1,130]{3,0,2,1:T(4,128)S(1)}, f32[4,10,1,130]{3,0,2,1:T(4,128)S(1)}, u32[]{:S(2)}, u32[]{:S(2)}) %collective-permute-start.40) | collective-permute-done | bytes 20832 | tf_op jit(solution)/shard_map/ppermute | solution.py:22
  286.9 4.2 %collective-permute-start.43 = (f32[4,1,32,128]{3,2,1,0:T(8,128)S(1)}, f32[4,1,32,128]{3,2,1,0:T(8,128)S(1)}, u32[]{:S(2)}, u32[]{:S(2)}) collective-permute-start(f32[4,1,32,128]{3,2,1,0:T(8,128)S(1)} %get-tuple-element.71), channel_id=1, source_target_pairs={{0,16},{16,32},{32,48},{48,64},{64,80},{80,96},{96,112},{1,17},{17... | collective-permute-start | bytes 196616 | tf_op jit(solution)/shard_map/ppermute | solution.py:21
  291.1 1.9 collective-permute-start.42
  293.1 3.6 %collective-permute-done.42 = f32[4,1,32,128]{3,2,1,0:T(8,128)S(1)} collective-permute-done((f32[4,1,32,128]{3,2,1,0:T(8,128)S(1)}, f32[4,1,32,128]{3,2,1,0:T(8,128)S(1)}, u32[]{:S(2)}, u32[]{:S(2)}) %collective-permute-start.42) | collective-permute-done | bytes 65568 | tf_op jit(solution)/shard_map/ppermute | solution.py:22
  300.8 4.6 %collective-permute-start.44 = (f32[4,10,32,1]{2,0,3,1:T(4,128)S(1)}, f32[4,10,32,1]{2,0,3,1:T(4,128)S(1)}, u32[]{:S(2)}, u32[]{:S(2)}) collective-permute-start(f32[4,10,32,1]{2,0,3,1:T(4,128)S(1)} %copy.597), channel_id=1, source_target_pairs={{0,4},{4,8},{8,12},{1,5},{5,9},{9,13},{2,6},{6,10},{10,14},{3,7},{... | collective-permute-start | bytes 15368 | tf_op jit(solution)/shard_map/ppermute | solution.py:21
  306.9 3.1 collective-permute-start.47
  311.4 3.4 %collective-permute-done.46 = f32[4,10,1,130]{3,0,2,1:T(4,128)S(1)} collective-permute-done((f32[4,10,1,130]{3,0,2,1:T(4,128)S(1)}, f32[4,10,1,130]{3,0,2,1:T(4,128)S(1)}, u32[]{:S(2)}, u32[]{:S(2)}) %collective-permute-start.46) | collective-permute-done | bytes 20832 | tf_op jit(solution)/shard_map/ppermute | solution.py:22
  (277 shorter events, 77.9 us)
Async XLA Ops:
  1.7 24.4 %collective-permute-start.5 = (f32[5,8,2,128]{3,1,2,0:T(8,128)S(1)}, f32[5,8,2,128]{3,1,2,0:T(8,128)S(1)}, u32[]{:S(2)}, u32[]{:S(2)}) collective-permute-start(f32[5,8,2,128]{3,1,2,0:T(8,128)S(1)} %copy.594), channel_id=1, source_target_pairs={{1,0},{2,1},{3,2},{5,4},{6,5},{7,6},{9,8},{10,9},{11,10},{13,12},{... | collective-permute-start | bytes 122888 | tf_op jit(solution)/shard_map/ppermute | solution.py:36
  3.0 22.9 %collective-permute-start = (f32[5,8,2,128]{3,1,2,0:T(8,128)S(1)}, f32[5,8,2,128]{3,1,2,0:T(8,128)S(1)}, u32[]{:S(2)}, u32[]{:S(2)}) collective-permute-start(f32[5,8,2,128]{3,1,2,0:T(8,128)S(1)} %copy.591), channel_id=1, source_target_pairs={{0,1},{1,2},{2,3},{4,5},{5,6},{6,7},{8,9},{9,10},{10,11},{12,13},{... | collective-permute-start | bytes 122888 | tf_op jit(solution)/shard_map/ppermute | solution.py:35
  8.8 17.5 %collective-permute-start.2 = (f32[5,2,32,128]{3,2,1,0:T(8,128)S(1)}, f32[5,2,32,128]{3,2,1,0:T(8,128)S(1)}, u32[]{:S(2)}, u32[]{:S(2)}) collective-permute-start(f32[5,2,32,128]{3,2,1,0:T(8,128)S(1)} %get-tuple-element.69), channel_id=1, source_target_pairs={{0,16},{16,32},{32,48},{48,64},{64,80},{80,96},{96,112},{1,17},{17... | collective-permute-start | bytes 491528 | tf_op jit(solution)/shard_map/ppermute | solution.py:35
  13.4 13.0 %collective-permute-start.3 = (f32[5,2,32,128]{3,2,1,0:T(8,128)S(1)}, f32[5,2,32,128]{3,2,1,0:T(8,128)S(1)}, u32[]{:S(2)}, u32[]{:S(2)}) collective-permute-start(f32[5,2,32,128]{3,2,1,0:T(8,128)S(1)} %get-tuple-element.70), channel_id=1, source_target_pairs={{16,0},{32,16},{48,32},{64,48},{80,64},{96,80},{112,96},{17,1},{33... | collective-permute-start | bytes 491528 | tf_op jit(solution)/shard_map/ppermute | solution.py:36
  15.8 4.6 %collective-permute-start.1 = (f32[5,8,32,2]{2,1,3,0:T(8,128)S(1)}, f32[5,8,32,2]{2,1,3,0:T(8,128)S(1)}, u32[]{:S(2)}, u32[]{:S(2)}) collective-permute-start(f32[5,8,32,2]{2,1,3,0:T(8,128)S(1)} %copy.592), channel_id=1, source_target_pairs={{0,4},{4,8},{8,12},{1,5},{5,9},{9,13},{2,6},{6,10},{10,14},{3,7},{... | collective-permute-start | bytes 30728 | tf_op jit(solution)/shard_map/ppermute | solution.py:35
  20.5 5.0 %collective-permute-start.4 = (f32[5,8,32,2]{2,1,3,0:T(8,128)S(1)}, f32[5,8,32,2]{2,1,3,0:T(8,128)S(1)}, u32[]{:S(2)}, u32[]{:S(2)}) collective-permute-start(f32[5,8,32,2]{2,1,3,0:T(8,128)S(1)} %copy.593), channel_id=1, source_target_pairs={{4,0},{8,4},{12,8},{5,1},{9,5},{13,9},{6,2},{10,6},{14,10},{7,3},{... | collective-permute-start | bytes 30728 | tf_op jit(solution)/shard_map/ppermute | solution.py:36
  31.8 7.6 %collective-permute-start.7 = (f32[4,1,32,128]{3,2,1,0:T(8,128)S(1)}, f32[4,1,32,128]{3,2,1,0:T(8,128)S(1)}, u32[]{:S(2)}, u32[]{:S(2)}) collective-permute-start(f32[4,1,32,128]{3,2,1,0:T(8,128)S(1)} %get-tuple-element.77), channel_id=1, source_target_pairs={{0,16},{16,32},{32,48},{48,64},{64,80},{80,96},{96,112},{1,17},{17... | collective-permute-start | bytes 196616 | tf_op jit(solution)/shard_map/ppermute | solution.py:21
  37.5 5.6 %collective-permute-start.6 = (f32[4,1,32,128]{3,2,1,0:T(8,128)S(1)}, f32[4,1,32,128]{3,2,1,0:T(8,128)S(1)}, u32[]{:S(2)}, u32[]{:S(2)}) collective-permute-start(f32[4,1,32,128]{3,2,1,0:T(8,128)S(1)} %get-tuple-element.78), channel_id=1, source_target_pairs={{16,0},{32,16},{48,32},{64,48},{80,64},{96,80},{112,96},{17,1},{33... | collective-permute-start | bytes 196616 | tf_op jit(solution)/shard_map/ppermute | solution.py:22
  45.6 5.9 %collective-permute-start.9 = (f32[4,10,32,1]{2,0,3,1:T(4,128)S(1)}, f32[4,10,32,1]{2,0,3,1:T(4,128)S(1)}, u32[]{:S(2)}, u32[]{:S(2)}) collective-permute-start(f32[4,10,32,1]{2,0,3,1:T(4,128)S(1)} %copy.596), channel_id=1, source_target_pairs={{4,0},{8,4},{12,8},{5,1},{9,5},{13,9},{6,2},{10,6},{14,10},{7,3},{... | collective-permute-start | bytes 15368 | tf_op jit(solution)/shard_map/ppermute | solution.py:22
  47.2 5.2 %collective-permute-start.8 = (f32[4,10,32,1]{2,0,3,1:T(4,128)S(1)}, f32[4,10,32,1]{2,0,3,1:T(4,128)S(1)}, u32[]{:S(2)}, u32[]{:S(2)}) collective-permute-start(f32[4,10,32,1]{2,0,3,1:T(4,128)S(1)} %copy.595), channel_id=1, source_target_pairs={{0,4},{4,8},{8,12},{1,5},{5,9},{9,13},{2,6},{6,10},{10,14},{3,7},{... | collective-permute-start | bytes 15368 | tf_op jit(solution)/shard_map/ppermute | solution.py:21
  53.0 4.5 %collective-permute-start.11 = (f32[4,10,1,130]{3,0,2,1:T(4,128)S(1)}, f32[4,10,1,130]{3,0,2,1:T(4,128)S(1)}, u32[]{:S(2)}, u32[]{:S(2)}) collective-permute-start(f32[4,10,1,130]{3,0,2,1:T(4,128)S(1)} %copy.546), channel_id=1, source_target_pairs={{0,1},{1,2},{2,3},{4,5},{5,6},{6,7},{8,9},{9,10},{10,11},{12,13},{... | collective-permute-start | bytes 62408 | tf_op jit(solution)/shard_map/ppermute | solution.py:21
  56.2 4.7 %collective-permute-start.10 = (f32[4,10,1,130]{3,0,2,1:T(4,128)S(1)}, f32[4,10,1,130]{3,0,2,1:T(4,128)S(1)}, u32[]{:S(2)}, u32[]{:S(2)}) collective-permute-start(f32[4,10,1,130]{3,0,2,1:T(4,128)S(1)} %copy.544), channel_id=1, source_target_pairs={{1,0},{2,1},{3,2},{5,4},{6,5},{7,6},{9,8},{10,9},{11,10},{13,12},{... | collective-permute-start | bytes 62408 | tf_op jit(solution)/shard_map/ppermute | solution.py:22
  63.8 6.2 %collective-permute-start.13 = (f32[4,1,32,128]{3,2,1,0:T(8,128)S(1)}, f32[4,1,32,128]{3,2,1,0:T(8,128)S(1)}, u32[]{:S(2)}, u32[]{:S(2)}) collective-permute-start(f32[4,1,32,128]{3,2,1,0:T(8,128)S(1)} %get-tuple-element.75), channel_id=1, source_target_pairs={{0,16},{16,32},{32,48},{48,64},{64,80},{80,96},{96,112},{1,17},{17... | collective-permute-start | bytes 196616 | tf_op jit(solution)/shard_map/ppermute | solution.py:21
  68.0 5.6 %collective-permute-start.12 = (f32[4,1,32,128]{3,2,1,0:T(8,128)S(1)}, f32[4,1,32,128]{3,2,1,0:T(8,128)S(1)}, u32[]{:S(2)}, u32[]{:S(2)}) collective-permute-start(f32[4,1,32,128]{3,2,1,0:T(8,128)S(1)} %get-tuple-element.76), channel_id=1, source_target_pairs={{16,0},{32,16},{48,32},{64,48},{80,64},{96,80},{112,96},{17,1},{33... | collective-permute-start | bytes 196616 | tf_op jit(solution)/shard_map/ppermute | solution.py:22
  76.1 30.4 %collective-permute-start.14 = (f32[4,10,32,1]{2,0,3,1:T(4,128)S(1)}, f32[4,10,32,1]{2,0,3,1:T(4,128)S(1)}, u32[]{:S(2)}, u32[]{:S(2)}) collective-permute-start(f32[4,10,32,1]{2,0,3,1:T(4,128)S(1)} %copy.552), channel_id=1, source_target_pairs={{0,4},{4,8},{8,12},{1,5},{5,9},{9,13},{2,6},{6,10},{10,14},{3,7},{... | collective-permute-start | bytes 15368 | tf_op jit(solution)/shard_map/ppermute | solution.py:21
  80.3 26.6 %collective-permute-start.15 = (f32[4,10,32,1]{2,0,3,1:T(4,128)S(1)}, f32[4,10,32,1]{2,0,3,1:T(4,128)S(1)}, u32[]{:S(2)}, u32[]{:S(2)}) collective-permute-start(f32[4,10,32,1]{2,0,3,1:T(4,128)S(1)} %copy.553), channel_id=1, source_target_pairs={{4,0},{8,4},{12,8},{5,1},{9,5},{13,9},{6,2},{10,6},{14,10},{7,3},{... | collective-permute-start | bytes 15368 | tf_op jit(solution)/shard_map/ppermute | solution.py:22
  107.6 5.3 %collective-permute-start.16 = (f32[4,10,1,130]{3,0,2,1:T(4,128)S(1)}, f32[4,10,1,130]{3,0,2,1:T(4,128)S(1)}, u32[]{:S(2)}, u32[]{:S(2)}) collective-permute-start(f32[4,10,1,130]{3,0,2,1:T(4,128)S(1)} %copy.556), channel_id=1, source_target_pairs={{1,0},{2,1},{3,2},{5,4},{6,5},{7,6},{9,8},{10,9},{11,10},{13,12},{... | collective-permute-start | bytes 62408 | tf_op jit(solution)/shard_map/ppermute | solution.py:22
  108.9 5.1 %collective-permute-start.17 = (f32[4,10,1,130]{3,0,2,1:T(4,128)S(1)}, f32[4,10,1,130]{3,0,2,1:T(4,128)S(1)}, u32[]{:S(2)}, u32[]{:S(2)}) collective-permute-start(f32[4,10,1,130]{3,0,2,1:T(4,128)S(1)} %copy.558), channel_id=1, source_target_pairs={{0,1},{1,2},{2,3},{4,5},{5,6},{6,7},{8,9},{9,10},{10,11},{12,13},{... | collective-permute-start | bytes 62408 | tf_op jit(solution)/shard_map/ppermute | solution.py:21
  172.0 24.3 %collective-permute-start.22 = (f32[4,4,1,64]{3,2,1,0:T(1,128)S(1)}, f32[4,4,1,64]{3,2,1,0:T(1,128)S(1)}, u32[]{:S(2)}, u32[]{:S(2)}) collective-permute-start(f32[4,4,1,64]{3,2,1,0:T(1,128)S(1)} %get-tuple-element.122), channel_id=1, source_target_pairs={{1,0},{2,1},{3,2},{5,4},{6,5},{7,6},{9,8},{10,9},{11,10},{13,12},{... | collective-permute-start | bytes 12296 | tf_op jit(solution)/shard_map/ppermute | solution.py:36
  173.3 23.1 %collective-permute-start.23 = (f32[4,4,1,64]{3,2,1,0:T(1,128)S(1)}, f32[4,4,1,64]{3,2,1,0:T(1,128)S(1)}, u32[]{:S(2)}, u32[]{:S(2)}) collective-permute-start(f32[4,4,1,64]{3,2,1,0:T(1,128)S(1)} %get-tuple-element.123), channel_id=1, source_target_pairs={{0,1},{1,2},{2,3},{4,5},{5,6},{6,7},{8,9},{9,10},{10,11},{12,13},{... | collective-permute-start | bytes 12296 | tf_op jit(solution)/shard_map/ppermute | solution.py:35
  177.6 18.9 %collective-permute-start.19 = (f32[4,1,16,64]{3,2,1,0:T(8,128)S(1)}, f32[4,1,16,64]{3,2,1,0:T(8,128)S(1)}, u32[]{:S(2)}, u32[]{:S(2)}) collective-permute-start(f32[4,1,16,64]{3,2,1,0:T(8,128)S(1)} %get-tuple-element.126), channel_id=1, source_target_pairs={{0,16},{16,32},{32,48},{48,64},{64,80},{80,96},{96,112},{1,17},{17... | collective-permute-start | bytes 49160 | tf_op jit(solution)/shard_map/ppermute | solution.py:35
  181.7 14.8 %collective-permute-start.18 = (f32[4,1,16,64]{3,2,1,0:T(8,128)S(1)}, f32[4,1,16,64]{3,2,1,0:T(8,128)S(1)}, u32[]{:S(2)}, u32[]{:S(2)}) collective-permute-start(f32[4,1,16,64]{3,2,1,0:T(8,128)S(1)} %get-tuple-element.127), channel_id=1, source_target_pairs={{16,0},{32,16},{48,32},{64,48},{80,64},{96,80},{112,96},{17,1},{33... | collective-permute-start | bytes 49160 | tf_op jit(solution)/shard_map/ppermute | solution.py:36
  183.7 6.6 %collective-permute-start.21 = (f32[4,4,16,1]{3,2,1,0:T(8,128)S(1)}, f32[4,4,16,1]{3,2,1,0:T(8,128)S(1)}, u32[]{:S(2)}, u32[]{:S(2)}) collective-permute-start(f32[4,4,16,1]{3,2,1,0:T(8,128)S(1)} %get-tuple-element.124), channel_id=1, source_target_pairs={{4,0},{8,4},{12,8},{5,1},{9,5},{13,9},{6,2},{10,6},{14,10},{7,3},{... | collective-permute-start | bytes 3080 | tf_op jit(solution)/shard_map/ppermute | solution.py:36
  190.4 6.0 %collective-permute-start.20 = (f32[4,4,16,1]{3,2,1,0:T(8,128)S(1)}, f32[4,4,16,1]{3,2,1,0:T(8,128)S(1)}, u32[]{:S(2)}, u32[]{:S(2)}) collective-permute-start(f32[4,4,16,1]{3,2,1,0:T(8,128)S(1)} %get-tuple-element.125), channel_id=1, source_target_pairs={{0,4},{4,8},{8,12},{1,5},{5,9},{9,13},{2,6},{6,10},{10,14},{3,7},{... | collective-permute-start | bytes 3080 | tf_op jit(solution)/shard_map/ppermute | solution.py:35
  197.3 25.3 %collective-permute-start.28 = (f32[4,4,1,64]{3,2,1,0:T(1,128)S(1)}, f32[4,4,1,64]{3,2,1,0:T(1,128)S(1)}, u32[]{:S(2)}, u32[]{:S(2)}) collective-permute-start(f32[4,4,1,64]{3,2,1,0:T(1,128)S(1)} %get-tuple-element.116), channel_id=1, source_target_pairs={{1,0},{2,1},{3,2},{5,4},{6,5},{7,6},{9,8},{10,9},{11,10},{13,12},{... | collective-permute-start | bytes 12296 | tf_op jit(solution)/shard_map/ppermute | solution.py:36
  198.6 24.1 %collective-permute-start.29 = (f32[4,4,1,64]{3,2,1,0:T(1,128)S(1)}, f32[4,4,1,64]{3,2,1,0:T(1,128)S(1)}, u32[]{:S(2)}, u32[]{:S(2)}) collective-permute-start(f32[4,4,1,64]{3,2,1,0:T(1,128)S(1)} %get-tuple-element.117), channel_id=1, source_target_pairs={{0,1},{1,2},{2,3},{4,5},{5,6},{6,7},{8,9},{9,10},{10,11},{12,13},{... | collective-permute-start | bytes 12296 | tf_op jit(solution)/shard_map/ppermute | solution.py:35
  202.6 20.2 %collective-permute-start.25 = (f32[4,1,16,64]{3,2,1,0:T(8,128)S(1)}, f32[4,1,16,64]{3,2,1,0:T(8,128)S(1)}, u32[]{:S(2)}, u32[]{:S(2)}) collective-permute-start(f32[4,1,16,64]{3,2,1,0:T(8,128)S(1)} %get-tuple-element.120), channel_id=1, source_target_pairs={{0,16},{16,32},{32,48},{48,64},{64,80},{80,96},{96,112},{1,17},{17... | collective-permute-start | bytes 49160 | tf_op jit(solution)/shard_map/ppermute | solution.py:35
  208.8 14.0 %collective-permute-start.24 = (f32[4,1,16,64]{3,2,1,0:T(8,128)S(1)}, f32[4,1,16,64]{3,2,1,0:T(8,128)S(1)}, u32[]{:S(2)}, u32[]{:S(2)}) collective-permute-start(f32[4,1,16,64]{3,2,1,0:T(8,128)S(1)} %get-tuple-element.121), channel_id=1, source_target_pairs={{16,0},{32,16},{48,32},{64,48},{80,64},{96,80},{112,96},{17,1},{33... | collective-permute-start | bytes 49160 | tf_op jit(solution)/shard_map/ppermute | solution.py:36
  210.9 6.4 %collective-permute-start.27 = (f32[4,4,16,1]{3,2,1,0:T(8,128)S(1)}, f32[4,4,16,1]{3,2,1,0:T(8,128)S(1)}, u32[]{:S(2)}, u32[]{:S(2)}) collective-permute-start(f32[4,4,16,1]{3,2,1,0:T(8,128)S(1)} %get-tuple-element.118), channel_id=1, source_target_pairs={{4,0},{8,4},{12,8},{5,1},{9,5},{13,9},{6,2},{10,6},{14,10},{7,3},{... | collective-permute-start | bytes 3080 | tf_op jit(solution)/shard_map/ppermute | solution.py:36
  217.3 5.3 %collective-permute-start.26 = (f32[4,4,16,1]{3,2,1,0:T(8,128)S(1)}, f32[4,4,16,1]{3,2,1,0:T(8,128)S(1)}, u32[]{:S(2)}, u32[]{:S(2)}) collective-permute-start(f32[4,4,16,1]{3,2,1,0:T(8,128)S(1)} %get-tuple-element.119), channel_id=1, source_target_pairs={{0,4},{4,8},{8,12},{1,5},{5,9},{9,13},{2,6},{6,10},{10,14},{3,7},{... | collective-permute-start | bytes 3080 | tf_op jit(solution)/shard_map/ppermute | solution.py:35
  223.6 25.1 %collective-permute-start.35 = (f32[4,4,1,64]{3,2,1,0:T(1,128)S(1)}, f32[4,4,1,64]{3,2,1,0:T(1,128)S(1)}, u32[]{:S(2)}, u32[]{:S(2)}) collective-permute-start(f32[4,4,1,64]{3,2,1,0:T(1,128)S(1)} %get-tuple-element.110), channel_id=1, source_target_pairs={{0,1},{1,2},{2,3},{4,5},{5,6},{6,7},{8,9},{9,10},{10,11},{12,13},{... | collective-permute-start | bytes 12296 | tf_op jit(solution)/shard_map/ppermute | solution.py:35
  227.2 21.5 %collective-permute-start.34 = (f32[4,4,1,64]{3,2,1,0:T(1,128)S(1)}, f32[4,4,1,64]{3,2,1,0:T(1,128)S(1)}, u32[]{:S(2)}, u32[]{:S(2)}) collective-permute-start(f32[4,4,1,64]{3,2,1,0:T(1,128)S(1)} %get-tuple-element.111), channel_id=1, source_target_pairs={{1,0},{2,1},{3,2},{5,4},{6,5},{7,6},{9,8},{10,9},{11,10},{13,12},{... | collective-permute-start | bytes 12296 | tf_op jit(solution)/shard_map/ppermute | solution.py:36
  228.5 20.3 %collective-permute-start.31 = (f32[4,1,16,64]{3,2,1,0:T(8,128)S(1)}, f32[4,1,16,64]{3,2,1,0:T(8,128)S(1)}, u32[]{:S(2)}, u32[]{:S(2)}) collective-permute-start(f32[4,1,16,64]{3,2,1,0:T(8,128)S(1)} %get-tuple-element.114), channel_id=1, source_target_pairs={{0,16},{16,32},{32,48},{48,64},{64,80},{80,96},{96,112},{1,17},{17... | collective-permute-start | bytes 49160 | tf_op jit(solution)/shard_map/ppermute | solution.py:35
  234.5 14.4 %collective-permute-start.30 = (f32[4,1,16,64]{3,2,1,0:T(8,128)S(1)}, f32[4,1,16,64]{3,2,1,0:T(8,128)S(1)}, u32[]{:S(2)}, u32[]{:S(2)}) collective-permute-start(f32[4,1,16,64]{3,2,1,0:T(8,128)S(1)} %get-tuple-element.115), channel_id=1, source_target_pairs={{16,0},{32,16},{48,32},{64,48},{80,64},{96,80},{112,96},{17,1},{33... | collective-permute-start | bytes 49160 | tf_op jit(solution)/shard_map/ppermute | solution.py:36
  236.5 6.0 %collective-permute-start.32 = (f32[4,4,16,1]{3,2,1,0:T(8,128)S(1)}, f32[4,4,16,1]{3,2,1,0:T(8,128)S(1)}, u32[]{:S(2)}, u32[]{:S(2)}) collective-permute-start(f32[4,4,16,1]{3,2,1,0:T(8,128)S(1)} %get-tuple-element.112), channel_id=1, source_target_pairs={{0,4},{4,8},{8,12},{1,5},{5,9},{9,13},{2,6},{6,10},{10,14},{3,7},{... | collective-permute-start | bytes 3080 | tf_op jit(solution)/shard_map/ppermute | solution.py:35
  242.5 6.1 %collective-permute-start.33 = (f32[4,4,16,1]{3,2,1,0:T(8,128)S(1)}, f32[4,4,16,1]{3,2,1,0:T(8,128)S(1)}, u32[]{:S(2)}, u32[]{:S(2)}) collective-permute-start(f32[4,4,16,1]{3,2,1,0:T(8,128)S(1)} %get-tuple-element.113), channel_id=1, source_target_pairs={{4,0},{8,4},{12,8},{5,1},{9,5},{13,9},{6,2},{10,6},{14,10},{7,3},{... | collective-permute-start | bytes 3080 | tf_op jit(solution)/shard_map/ppermute | solution.py:36
  253.9 7.6 %collective-permute-start.37 = (f32[4,1,32,128]{3,2,1,0:T(8,128)S(1)}, f32[4,1,32,128]{3,2,1,0:T(8,128)S(1)}, u32[]{:S(2)}, u32[]{:S(2)}) collective-permute-start(f32[4,1,32,128]{3,2,1,0:T(8,128)S(1)} %get-tuple-element.73), channel_id=1, source_target_pairs={{0,16},{16,32},{32,48},{48,64},{64,80},{80,96},{96,112},{1,17},{17... | collective-permute-start | bytes 196616 | tf_op jit(solution)/shard_map/ppermute | solution.py:21
  259.6 5.6 %collective-permute-start.36 = (f32[4,1,32,128]{3,2,1,0:T(8,128)S(1)}, f32[4,1,32,128]{3,2,1,0:T(8,128)S(1)}, u32[]{:S(2)}, u32[]{:S(2)}) collective-permute-start(f32[4,1,32,128]{3,2,1,0:T(8,128)S(1)} %get-tuple-element.74), channel_id=1, source_target_pairs={{16,0},{32,16},{48,32},{64,48},{80,64},{96,80},{112,96},{17,1},{33... | collective-permute-start | bytes 196616 | tf_op jit(solution)/shard_map/ppermute | solution.py:22
  267.7 5.9 %collective-permute-start.39 = (f32[4,10,32,1]{2,0,3,1:T(4,128)S(1)}, f32[4,10,32,1]{2,0,3,1:T(4,128)S(1)}, u32[]{:S(2)}, u32[]{:S(2)}) collective-permute-start(f32[4,10,32,1]{2,0,3,1:T(4,128)S(1)} %copy.568), channel_id=1, source_target_pairs={{4,0},{8,4},{12,8},{5,1},{9,5},{13,9},{6,2},{10,6},{14,10},{7,3},{... | collective-permute-start | bytes 15368 | tf_op jit(solution)/shard_map/ppermute | solution.py:22
  269.3 5.2 %collective-permute-start.38 = (f32[4,10,32,1]{2,0,3,1:T(4,128)S(1)}, f32[4,10,32,1]{2,0,3,1:T(4,128)S(1)}, u32[]{:S(2)}, u32[]{:S(2)}) collective-permute-start(f32[4,10,32,1]{2,0,3,1:T(4,128)S(1)} %copy.567), channel_id=1, source_target_pairs={{0,4},{4,8},{8,12},{1,5},{5,9},{9,13},{2,6},{6,10},{10,14},{3,7},{... | collective-permute-start | bytes 15368 | tf_op jit(solution)/shard_map/ppermute | solution.py:21
  275.1 5.6 %collective-permute-start.41 = (f32[4,10,1,130]{3,0,2,1:T(4,128)S(1)}, f32[4,10,1,130]{3,0,2,1:T(4,128)S(1)}, u32[]{:S(2)}, u32[]{:S(2)}) collective-permute-start(f32[4,10,1,130]{3,0,2,1:T(4,128)S(1)} %copy.573), channel_id=1, source_target_pairs={{0,1},{1,2},{2,3},{4,5},{5,6},{6,7},{8,9},{9,10},{10,11},{12,13},{... | collective-permute-start | bytes 62408 | tf_op jit(solution)/shard_map/ppermute | solution.py:21
  279.4 4.7 %collective-permute-start.40 = (f32[4,10,1,130]{3,0,2,1:T(4,128)S(1)}, f32[4,10,1,130]{3,0,2,1:T(4,128)S(1)}, u32[]{:S(2)}, u32[]{:S(2)}) collective-permute-start(f32[4,10,1,130]{3,0,2,1:T(4,128)S(1)} %copy.571), channel_id=1, source_target_pairs={{1,0},{2,1},{3,2},{5,4},{6,5},{7,6},{9,8},{10,9},{11,10},{13,12},{... | collective-permute-start | bytes 62408 | tf_op jit(solution)/shard_map/ppermute | solution.py:22
  286.9 6.1 %collective-permute-start.43 = (f32[4,1,32,128]{3,2,1,0:T(8,128)S(1)}, f32[4,1,32,128]{3,2,1,0:T(8,128)S(1)}, u32[]{:S(2)}, u32[]{:S(2)}) collective-permute-start(f32[4,1,32,128]{3,2,1,0:T(8,128)S(1)} %get-tuple-element.71), channel_id=1, source_target_pairs={{0,16},{16,32},{32,48},{48,64},{64,80},{80,96},{96,112},{1,17},{17... | collective-permute-start | bytes 196616 | tf_op jit(solution)/shard_map/ppermute | solution.py:21
  291.1 5.6 %collective-permute-start.42 = (f32[4,1,32,128]{3,2,1,0:T(8,128)S(1)}, f32[4,1,32,128]{3,2,1,0:T(8,128)S(1)}, u32[]{:S(2)}, u32[]{:S(2)}) collective-permute-start(f32[4,1,32,128]{3,2,1,0:T(8,128)S(1)} %get-tuple-element.72), channel_id=1, source_target_pairs={{16,0},{32,16},{48,32},{64,48},{80,64},{96,80},{112,96},{17,1},{33... | collective-permute-start | bytes 196616 | tf_op jit(solution)/shard_map/ppermute | solution.py:22
  299.2 6.2 %collective-permute-start.45 = (f32[4,10,32,1]{2,0,3,1:T(4,128)S(1)}, f32[4,10,32,1]{2,0,3,1:T(4,128)S(1)}, u32[]{:S(2)}, u32[]{:S(2)}) collective-permute-start(f32[4,10,32,1]{2,0,3,1:T(4,128)S(1)} %copy.598), channel_id=1, source_target_pairs={{4,0},{8,4},{12,8},{5,1},{9,5},{13,9},{6,2},{10,6},{14,10},{7,3},{... | collective-permute-start | bytes 15368 | tf_op jit(solution)/shard_map/ppermute | solution.py:22
  300.8 5.5 %collective-permute-start.44 = (f32[4,10,32,1]{2,0,3,1:T(4,128)S(1)}, f32[4,10,32,1]{2,0,3,1:T(4,128)S(1)}, u32[]{:S(2)}, u32[]{:S(2)}) collective-permute-start(f32[4,10,32,1]{2,0,3,1:T(4,128)S(1)} %copy.597), channel_id=1, source_target_pairs={{0,4},{4,8},{8,12},{1,5},{5,9},{9,13},{2,6},{6,10},{10,14},{3,7},{... | collective-permute-start | bytes 15368 | tf_op jit(solution)/shard_map/ppermute | solution.py:21
  306.9 4.4 %collective-permute-start.47 = (f32[4,10,1,130]{3,0,2,1:T(4,128)S(1)}, f32[4,10,1,130]{3,0,2,1:T(4,128)S(1)}, u32[]{:S(2)}, u32[]{:S(2)}) collective-permute-start(f32[4,10,1,130]{3,0,2,1:T(4,128)S(1)} %copy.585), channel_id=1, source_target_pairs={{0,1},{1,2},{2,3},{4,5},{5,6},{6,7},{8,9},{9,10},{10,11},{12,13},{... | collective-permute-start | bytes 62408 | tf_op jit(solution)/shard_map/ppermute | solution.py:21
  310.1 4.7 %collective-permute-start.46 = (f32[4,10,1,130]{3,0,2,1:T(4,128)S(1)}, f32[4,10,1,130]{3,0,2,1:T(4,128)S(1)}, u32[]{:S(2)}, u32[]{:S(2)}) collective-permute-start(f32[4,10,1,130]{3,0,2,1:T(4,128)S(1)} %copy.583), channel_id=1, source_target_pairs={{1,0},{2,1},{3,2},{5,4},{6,5},{7,6},{9,8},{10,9},{11,10},{13,12},{... | collective-permute-start | bytes 62408 | tf_op jit(solution)/shard_map/ppermute | solution.py:22
  (46 other events, 342.4 us)
where the time goes:
time: 321 us; the launch traced here: 319 us
  starting transfers between devices  140 us (44%)
  local copies, waits for them, and re-layouts  80.4 us (25%)
  waiting for transfers between devices  52.6 us (16%)
  other arithmetic  43.5 us (14%)
    ppermute x12, starting transfers between devices, extended(): lax.ppermute(last, axis, up)  52.2 us
    ppermute x12, starting transfers between devices, padded_2(): before = lax.ppermute(last, axis, up)  51.1 us
    concatenate x3, local copies, waits for them, and re-layouts, local(): jnp.concatenate([momentum, continuity[None], viscosity[None]], axis=0)  47.5 us
    ppermute x12, waiting for transfers between devices, padded_2(): after = lax.ppermute(first, axis, down)  24.7 us
    reduce_sum x2, other arithmetic, restrict(): return blocks.mean(axis=(2, 4, 6))  22.1 us
    ppermute x12, waiting for transfers between devices, extended(): lax.ppermute(first, axis, [(b, a) for a, b in up])  18.6 us
    ppermute x12, starting transfers between devices, padded_2(): after = lax.ppermute(first, axis, down)  18.3 us
    ppermute x12, starting transfers between devices, extended(): lax.ppermute(first, axis, [(b, a) for a, b in up])  18 us
  transfers between devices with their start and end apart: 48, of which 19 were waited for; matrix products, arithmetic and copies ran while one was open for 10% of the time, Pallas kernels for 0%

commit v1 on v0

v1 whole, which is shorter than its diff:
```python
import functools

import jax
import jax.numpy as jnp
from jax import lax
from jax.experimental import pallas as pl
from jax.experimental.pallas import tpu as pltpu
from jax.sharding import PartitionSpec as P

MESH = pl.DeviceIdType.MESH
F32 = jnp.float32
NX, NZ, NY = 8, 32, 128
CX, CZ = 4, 16
TOP = 8
AXES = ("gx", "gz", "gy")


def kernel(
    size, vel, prs, vis, frc, vout, pout,
    u0, u1, u2, u3, u4, visc, force, cvisc, c1, c2, c3,
    wts, scl, diag, rhs, cwts, cscl, crhs, tmp, out,
    ysend0, yrecv0, ysend, yrecv, csend, crecv,
    send_sem, recv_sem, load_sem, store_sem,
):
    where = {axis: lax.axis_index(axis) for axis in AXES}
    lane = lax.broadcasted_iota(jnp.int32, (8, NY), 1)
    even = lax.rem(lane, 2) == 0
    count = [0]
    pending = []

    def roll(value, shift):
        return pltpu.roll(value, shift, 1)

    def neighbours(axis):
        n = size[axis]
        me = where[axis]
        return lax.rem(me + 1, n), lax.rem(me + n - 1, n), me < n - 1, me > 0

    def pair(axis, high_face, low_halo, low_face, high_halo):
        upper, lower, has_upper, has_lower = neighbours(axis)
        slot = count[0]
        count[0] += 2

        def make(k, src, dst, device):
            return pltpu.make_async_remote_copy(
                src_ref=src, dst_ref=dst,
                send_sem=send_sem.at[slot + k], recv_sem=recv_sem.at[slot + k],
                device_id={axis: device}, device_id_type=MESH,
            )

        def up():
            return make(0, high_face, low_halo, upper)

        def down():
            return make(1, low_face, high_halo, lower)

        def start():
            @pl.when(has_upper)
            def _():
                up().start()

            @pl.when(has_lower)
            def _():
                down().start()

        def wait():
            @pl.when(has_lower)
            def _():
                up().wait_recv()

            @pl.when(has_upper)
            def _():
                down().wait_recv()

        def drain():
            @pl.when(has_upper)
            def _():
                up().wait_send()

            @pl.when(has_lower)
            def _():
                down().wait_send()

        pending.append(drain)
        return start, wait

    zs = pl.ds(TOP, NZ)

    def x_pair(u, source=None):
        if source is None:
            high, low = u.at[:, NX, zs, :], u.at[:, 1, zs, :]
        else:
            high, low = source
        return pair("gx", high, u.at[:, 0, zs, :], low, u.at[:, NX + 1, zs, :])

    def z_pair(u):
        xs = pl.ds(1, NX)
        return pair(
            "gz", u.at[:, xs, TOP + NZ - 1, :], u.at[:, xs, TOP - 1, :],
            u.at[:, xs, TOP, :], u.at[:, xs, TOP + NZ, :],
        )

    def y_pair(sent, received):
        return pair("gy", sent.at[1], received.at[0], sent.at[0], received.at[1])

    fine_planes = pl.ds(1, NX)
    loads = [
        pltpu.make_async_copy(vel, u0.at[0:3, fine_planes, zs, :], load_sem.at[0]),
        pltpu.make_async_copy(prs, u0.at[3, fine_planes, zs, :], load_sem.at[1]),
        pltpu.make_async_copy(vis, visc.at[fine_planes, zs, :], load_sem.at[2]),
        pltpu.make_async_copy(frc, force, load_sem.at[3]),
    ]
    for load in loads:
        load.start()

    barrier = pltpu.get_barrier_semaphore()
    total = jnp.int32(0)
    for axis in AXES:
        upper, lower, has_upper, has_lower = neighbours(axis)
        for device, has in ((upper, has_upper), (lower, has_lower)):
            @pl.when(has)
            def _():
                pl.semaphore_signal(barrier, inc=1, device_id={axis: device}, device_id_type=MESH)
            total = total + has.astype(jnp.int32)
    pl.semaphore_wait(barrier, total)

    first = [
        pair("gx", vel.at[:, NX - 1], u0.at[0:3, 0, zs, :], vel.at[:, 0], u0.at[0:3, NX + 1, zs, :]),
        pair("gx", prs.at[NX - 1], u0.at[3, 0, zs, :], prs.at[0], u0.at[3, NX + 1, zs, :]),
        pair("gx", vis.at[NX - 1], visc.at[0, zs, :], vis.at[0], visc.at[NX + 1, zs, :]),
    ]
    for start, _ in first:
        start()

    def zero(ref):
        ref[...] = jnp.zeros(ref.shape, F32)

    def edges(axis, low, high):
        @pl.when(where[axis] == 0)
        def _():
            for ref in low:
                zero(ref)

        @pl.when(where[axis] == size[axis] - 1)
        def _():
            for ref in high:
                zero(ref)

    fields = (u0, u1, u2, u3, u4)
    coarse = (c1, c2, c3)
    czs, cxs = pl.ds(TOP, CZ), pl.ds(1, CX)
    edges(
        "gx",
        [u.at[:, 0, zs, :] for u in fields] + [visc.at[0, zs, :], cvisc.at[0, czs, :]]
        + [c.at[:, 0, czs, :] for c in coarse],
        [u.at[:, NX + 1, zs, :] for u in fields] + [visc.at[NX + 1, zs, :], cvisc.at[CX + 1, czs, :]]
        + [c.at[:, CX + 1, czs, :] for c in coarse],
    )
    edges(
        "gz",
        [u.at[:, fine_planes, TOP - 1 : TOP, :] for u in fields]
        + [visc.at[fine_planes, TOP - 1 : TOP, :], cvisc.at[cxs, TOP - 1 : TOP, :]]
        + [c.at[:, cxs, TOP - 1 : TOP, :] for c in coarse],
        [u.at[:, fine_planes, TOP + NZ : TOP + NZ + 1, :] for u in fields]
        + [visc.at[fine_planes, TOP + NZ : TOP + NZ + 1, :], cvisc.at[cxs, TOP + CZ : TOP + CZ + 1, :]]
        + [c.at[:, cxs, TOP + CZ : TOP + CZ + 1, :] for c in coarse],
    )
    edges(
        "gy",
        [yrecv0.at[0]] + [yrecv.at[s, 0] for s in range(4)] + [crecv.at[s, 0] for s in range(3)],
        [yrecv0.at[1]] + [yrecv.at[s, 1] for s in range(4)] + [crecv.at[s, 1] for s in range(3)],
    )

    for load in loads[:3]:
        load.wait()
    more = [
        z_pair(u0),
        pair(
            "gz", visc.at[fine_planes, TOP + NZ - 1, :], visc.at[fine_planes, TOP - 1, :],
            visc.at[fine_planes, TOP, :], visc.at[fine_planes, TOP + NZ, :],
        ),
    ]
    for start, _ in more:
        start()
    first += more

    def slot_of(k, i, t):
        return t * 32 + k * 8 + i

    def put(packs, value, slot):
        low, high = packs
        here = lane == slot
        low = jnp.where(here, roll(value, slot), low)
        high = jnp.where(here, roll(value, lax.rem(slot + 1, NY)), high)
        return low, high

    def y_shifts(value, packs, slot):
        low, high = packs
        before = jnp.where(lane == 0, roll(low, lax.rem(NY - slot, NY)), roll(value, 1))
        after = jnp.where(lane == NY - 1, roll(high, NY - 1 - slot), roll(value, NY - 1))
        return before, after

    nil = jnp.zeros((8, NY), F32)

    def cslot(k, i, t):
        return 2 * (t * 16 + k * 4 + i)

    def put2(packs, value, slot):
        low, high = packs
        here = (lane == slot) | (lane == slot + 1)
        low = jnp.where(here, roll(value, slot), low)
        high = jnp.where(here, roll(value, (slot + 2) % NY), high)
        return low, high

    def y_shifts2(value, packs, slot):
        low, high = packs
        before = jnp.where(lane < 2, roll(low, (NY - slot) % NY), roll(value, 2))
        after = jnp.where(lane >= NY - 2, roll(high, NY - 2 - slot), roll(value, NY - 2))
        return before, after

    def halves(i, t, source):
        return source[i, pl.ds(TOP + 8 * t, 8), :]

    def first_pack(i, carry):
        fields_pack, visc_pack = (carry[0], carry[1]), (carry[2], carry[3])
        for t in range(4):
            rows = pl.ds(TOP + 8 * t, 8)
            for k in range(4):
                fields_pack = put(fields_pack, u0[k, i + 1, rows, :], slot_of(k, i, t))
            visc_pack = put(visc_pack, visc[i + 1, rows, :], t * 8 + i)
        return (*fields_pack, *visc_pack)

    fl, fh, vl, vh = lax.fori_loop(0, NX, first_pack, (nil, nil, nil, nil))

    def pair_sum(value):
        return value + jnp.where(even, roll(value, NY - 1), roll(value, 1))

    def z_pairs(ref, t):
        return ref[pl.ds(16 * t, 8, stride=2), :] + ref[pl.ds(16 * t + 1, 8, stride=2), :]

    cpack = (vl, vh)
    for i in range(CX):
        for t in range(4):
            rows = pl.ds(TOP + 8 * t, 8)
            tmp[0, i, pl.ds(8 * t, 8), :] = pair_sum(visc[2 * i + 1, rows, :] + visc[2 * i + 2, rows, :])
        for t in range(2):
            mean = 0.125 * z_pairs(tmp.at[0, i], t)
            cvisc[i + 1, pl.ds(TOP + 8 * t, 8), :] = mean
            cpack = put2(cpack, mean, 64 + 2 * (t * 4 + i))
    ysend0[0, 0], ysend0[1, 0] = fl, fh
    ysend0[0, 1], ysend0[1, 1] = cpack
    more = [
        y_pair(ysend0, yrecv0),
        pair("gx", cvisc.at[CX, czs, :], cvisc.at[0, czs, :], cvisc.at[1, czs, :], cvisc.at[CX + 1, czs, :]),
        pair(
            "gz", cvisc.at[cxs, TOP + CZ - 1, :], cvisc.at[cxs, TOP - 1, :],
            cvisc.at[cxs, TOP, :], cvisc.at[cxs, TOP + CZ, :],
        ),
    ]
    for start, _ in more:
        start()
    first += more
    loads[3].wait()
    for _, wait in first:
        wait()

    def stencil_weights(here, around):
        sums = [here + other for other in around]
        twice = sums[0] + sums[1] + sums[2] + sums[3] + sums[4] + sums[5]
        scale = 0.6 / twice
        return scale, [scale * s for s in sums], twice

    def weights(i, _):
        packs = (yrecv0[0, 1], yrecv0[1, 1])
        for t in range(4):
            r = TOP + 8 * t
            here = visc[i + 1, pl.ds(r, 8), :]
            before, after = y_shifts(here, packs, t * 8 + i)
            around = (
                visc[i, pl.ds(r, 8), :], visc[i + 2, pl.ds(r, 8), :],
                visc[i + 1, pl.ds(r - 1, 8), :], visc[i + 1, pl.ds(r + 1, 8), :],
                before, after,
            )
            scale, sides, twice = stencil_weights(here, around)
            rows = pl.ds(8 * t, 8)
            for j in range(6):
                wts[j, i, rows, :] = sides[j]
            scl[i, rows, :] = scale
            diag[i, rows, :] = twice * (0.5 / 0.6)
            for k in range(3):
                rhs[k, i, rows, :] = (2.0 * scale) * force[k, i, rows, :]
        return 0

    def coarse_weights():
        packs = (yrecv0[0, 1], yrecv0[1, 1])
        for i in range(CX):
            for t in range(2):
                r = TOP + 8 * t
                here = cvisc[i + 1, pl.ds(r, 8), :]
                before, after = y_shifts2(here, packs, 64 + 2 * (t * 4 + i))
                around = (
                    cvisc[i, pl.ds(r, 8), :], cvisc[i + 2, pl.ds(r, 8), :],
                    cvisc[i + 1, pl.ds(r - 1, 8), :], cvisc[i + 1, pl.ds(r + 1, 8), :],
                    before, after,
                )
                scale, sides, _ = stencil_weights(here, around)
                rows = pl.ds(8 * t, 8)
                for j in range(6):
                    cwts[j, i, rows, :] = sides[j]
                cscl[i, rows, :] = scale

    lax.fori_loop(0, NX, weights, 0)

    def terms(here, around, sides, grad_scale):
        moves, spread = [], None
        for k in range(3):
            total = sides[0] * around[0][k]
            for j in range(1, 6):
                total = total + sides[j] * around[j][k]
            moves.append(total - grad_scale * (around[2 * k + 1][3] - around[2 * k][3]))
            d = around[2 * k + 1][k] - around[2 * k][k]
            spread = d if spread is None else spread + d
        return moves, spread

    def fine_terms(u, packs, i, t):
        r = TOP + 8 * t
        rows = pl.ds(8 * t, 8)
        here = [u[k, i + 1, pl.ds(r, 8), :] for k in range(4)]
        ys = [y_shifts(here[k], packs, slot_of(k, i, t)) for k in range(4)]
        around = (
            [u[k, i, pl.ds(r, 8), :] for k in range(4)],
            [u[k, i + 2, pl.ds(r, 8), :] for k in range(4)],
            [u[k, i + 1, pl.ds(r - 1, 8), :] for k in range(4)],
            [u[k, i + 1, pl.ds(r + 1, 8), :] for k in range(4)],
            [y[0] for y in ys],
            [y[1] for y in ys],
        )
        sides = [wts[j, i, rows, :] for j in range(6)]
        moves, spread = terms(here, around, sides, scl[i, rows, :])
        moves = [m + rhs[k, i, rows, :] for k, m in enumerate(moves)]
        return here, moves, spread

    def fine_update(u, packs, i, t):
        here, moves, spread = fine_terms(u, packs, i, t)
        new = [0.4 * here[k] + moves[k] for k in range(3)]
        new.append(here[3] - 0.25 * (visc[i + 1, pl.ds(TOP + 8 * t, 8), :] * spread))
        return new

    def order(j):
        return jnp.where(j == 1, NX - 1, jnp.maximum(j - 1, 0))

    def exchange(u, make, sent, received):
        def body(j, packs):
            i = order(j)
            for t in range(4):
                new = make(i, t)
                for k in range(4):
                    u[k, i + 1, pl.ds(TOP + 8 * t, 8), :] = new[k]
                    packs = put(packs, new[k], slot_of(k, i, t))
            return packs

        packs = lax.fori_loop(0, 2, body, (nil, nil))
        x_start, x_wait = x_pair(u)
        x_start()
        packs = lax.fori_loop(2, NX, body, packs)
        sent[0], sent[1] = packs
        z_start, z_wait = z_pair(u)
        z_start()
        y_start, y_wait = y_pair(sent, received)
        y_start()

        def wait():
            x_wait()
            z_wait()
            y_wait()

        return wait

    packs = (yrecv0[0, 0], yrecv0[1, 0])
    wait = exchange(u1, lambda i, t: fine_update(u0, packs, i, t), ysend.at[0], yrecv.at[0])
    coarse_weights()
    wait()
    packs1 = (yrecv[0, 0], yrecv[0, 1])
    wait = exchange(u2, lambda i, t: fine_update(u1, packs1, i, t), ysend.at[1], yrecv.at[1])
    wait()

    packs2 = (yrecv[1, 0], yrecv[1, 1])

    def restrict(i, _):
        for t in range(4):
            sums = None
            for h in range(2):
                here, moves, spread = fine_terms(u2, packs2, 2 * i + h, t)
                d = diag[2 * i + h, pl.ds(8 * t, 8), :]
                parts = [d * (moves[k] - 0.6 * here[k]) for k in range(3)] + [spread]
                sums = parts if sums is None else [a + b for a, b in zip(sums, parts)]
            for k in range(4):
                tmp[k, i, pl.ds(8 * t, 8), :] = pair_sum(sums[k])
        return 0

    lax.fori_loop(0, CX, restrict, 0)

    def coarse_exchange(c, values, sent, received):
        packs = (nil, nil)
        for i in (0, CX - 1, 1, CX - 2):
            for t in range(2):
                new = values(i, t)
                for k in range(4):
                    c[k, i + 1, pl.ds(TOP + 8 * t, 8), :] = new[k]
                    packs = put2(packs, new[k], cslot(k, i, t))
        sent[0], sent[1] = packs
        copies = [
            pair(
                "gx", c.at[:, CX, czs, :], c.at[:, 0, czs, :], c.at[:, 1, czs, :], c.at[:, CX + 1, czs, :],
            ),
            pair(
                "gz", c.at[:, cxs, TOP + CZ - 1, :], c.at[:, cxs, TOP - 1, :],
                c.at[:, cxs, TOP, :], c.at[:, cxs, TOP + CZ, :],
            ),
            y_pair(sent, received),
        ]
        for start, _ in copies:
            start()

        def wait():
            for _, one in copies:
                one()

        return wait

    def start_values(i, t):
        rows = pl.ds(8 * t, 8)
        scale = cscl[i, rows, :]
        new = [scale * z_pairs(tmp.at[k, i], t) for k in range(3)]
        new.append(-0.03125 * (cvisc[i + 1, pl.ds(TOP + 8 * t, 8), :] * z_pairs(tmp.at[3, i], t)))
        for k in range(4):
            crhs[k, i, rows, :] = new[k]
        return new

    def coarse_update(c, packs, i, t):
        r = TOP + 8 * t
        rows = pl.ds(8 * t, 8)
        here = [c[k, i + 1, pl.ds(r, 8), :] for k in range(4)]
        ys = [y_shifts2(here[k], packs, cslot(k, i, t)) for k in range(4)]
        around = (
            [c[k, i, pl.ds(r, 8), :] for k in range(4)],
            [c[k, i + 2, pl.ds(r, 8), :] for k in range(4)],
            [c[k, i + 1, pl.ds(r - 1, 8), :] for k in range(4)],
            [c[k, i + 1, pl.ds(r + 1, 8), :] for k in range(4)],
            [y[0] for y in ys],
            [y[1] for y in ys],
        )
        sides = [cwts[j, i, rows, :] for j in range(6)]
        moves, spread = terms(here, around, sides, 2.0 * cscl[i, rows, :])
        new = [0.4 * here[k] + (moves[k] + crhs[k, i, rows, :]) for k in range(3)]
        new.append(here[3] + (crhs[3, i, rows, :] - 0.125 * (cvisc[i + 1, pl.ds(r, 8), :] * spread)))
        return new

    wait = coarse_exchange(c1, start_values, csend.at[0], crecv.at[0])
    wait()
    cp1 = (crecv[0, 0], crecv[0, 1])
    wait = coarse_exchange(c2, lambda i, t: coarse_update(c1, cp1, i, t), csend.at[1], crecv.at[1])
    wait()
    cp2 = (crecv[1, 0], crecv[1, 1])
    wait = coarse_exchange(c3, lambda i, t: coarse_update(c2, cp2, i, t), csend.at[2], crecv.at[2])
    wait()
    cp3 = (crecv[2, 0], crecv[2, 1])
    for i in range(CX):
        for t in range(2):
            new = coarse_update(c3, cp3, i, t)
            for k in range(4):
                tmp[k, i, pl.ds(16 * t, 8, stride=2), :] = new[k]
                tmp[k, i, pl.ds(16 * t + 1, 8, stride=2), :] = new[k]

    def corrected(i, t):
        half = lax.div(i, 2)
        return [
            u2[k, i + 1, pl.ds(TOP + 8 * t, 8), :] + tmp[k, half, pl.ds(8 * t, 8), :] for k in range(4)
        ]

    wait = exchange(u3, corrected, ysend.at[2], yrecv.at[2])
    wait()
    packs3 = (yrecv[2, 0], yrecv[2, 1])
    wait = exchange(u4, lambda i, t: fine_update(u3, packs3, i, t), ysend.at[3], yrecv.at[3])
    wait()
    packs4 = (yrecv[3, 0], yrecv[3, 1])

    def stores(i):
        return (
            pltpu.make_async_copy(out.at[0:3, i], vout.at[:, i], store_sem.at[0, i]),
            pltpu.make_async_copy(out.at[3, i], pout.at[i], store_sem.at[1, i]),
        )

    def last(i, _):
        for t in range(4):
            new = fine_update(u4, packs4, i, t)
            for k in range(4):
                out[k, i, pl.ds(8 * t, 8), :] = new[k]
        for store in stores(i):
            store.start()
        return 0

    lax.fori_loop(0, NX, last, 0)
    for i in range(NX):
        for store in stores(i):
            store.wait()
    for drain in pending:
        drain()


COPIES = 2 * (3 + 2 + 3 + 4 * 3 + 3 * 3)


def cycle(size, velocity, pressure, viscosity, body_force):
    field = pltpu.VMEM((4, NX + 2, NZ + 16, NY), F32)
    small = pltpu.VMEM((4, CX + 2, CZ + 16, NY), F32)
    anywhere = pl.BlockSpec(memory_space=pl.ANY)
    out = pl.pallas_call(
        functools.partial(kernel, size),
        out_shape=(
            jax.ShapeDtypeStruct((3, NX, NZ, NY), F32),
            jax.ShapeDtypeStruct((NX, NZ, NY), F32),
        ),
        in_specs=[anywhere] * 4,
        out_specs=(anywhere, anywhere),
        scratch_shapes=[
            field, field, field, field, field,
            pltpu.VMEM((NX + 2, NZ + 16, NY), F32),
            pltpu.VMEM((3, NX, NZ, NY), F32),
            pltpu.VMEM((CX + 2, CZ + 16, NY), F32),
            small, small, small,
            pltpu.VMEM((6, NX, NZ, NY), F32),
            pltpu.VMEM((NX, NZ, NY), F32),
            pltpu.VMEM((NX, NZ, NY), F32),
            pltpu.VMEM((3, NX, NZ, NY), F32),
            pltpu.VMEM((6, CX, CZ, NY), F32),
            pltpu.VMEM((CX, CZ, NY), F32),
            pltpu.VMEM((4, CX, CZ, NY), F32),
            pltpu.VMEM((4, CX, NZ, NY), F32),
            pltpu.VMEM((4, NX, NZ, NY), F32),
            pltpu.VMEM((2, 2, 8, NY), F32),
            pltpu.VMEM((2, 2, 8, NY), F32),
            pltpu.VMEM((4, 2, 8, NY), F32),
            pltpu.VMEM((4, 2, 8, NY), F32),
            pltpu.VMEM((3, 2, 8, NY), F32),
            pltpu.VMEM((3, 2, 8, NY), F32),
            pltpu.SemaphoreType.DMA((COPIES,)),
            pltpu.SemaphoreType.DMA((COPIES,)),
            pltpu.SemaphoreType.DMA((4,)),
            pltpu.SemaphoreType.DMA((2, NX)),
        ],
        compiler_params=pltpu.CompilerParams(collective_id=0, has_side_effects=True),
        name="cycle",
    )(velocity, pressure, viscosity, body_force)
    return out[0], out[1]


def solution(mesh):
    return jax.shard_map(
        functools.partial(cycle, dict(mesh.shape)),
        mesh=mesh,
        in_specs=(
            P(None, "gx", "gz", "gy"),
            P("gx", "gz", "gy"),
            P("gx", "gz", "gy"),
            P(None, "gx", "gz", "gy"),
        ),
        out_specs=(P(None, "gx", "gz", "gy"), P("gx", "gz", "gy")),
        check_vma=False,
    )
```

time: 321 us -> 44 us (0.14)
  starting transfers between devices: 140 us -> 0 us
  local copies, waits for them, and re-layouts: 80.4 us -> 2.46 us
  waiting for transfers between devices: 52.6 us -> 0 us
  other arithmetic: 43.5 us -> 0 us
  Pallas kernels: 0 us -> 40.7 us
    ppermute x48 -> x0, starting transfers between devices: 140 us -> none  [the longest x12 52.2 us: extended(): lax.ppermute(last, axis, up)]
    ppermute x48 -> x0, waiting for transfers between devices: 52.6 us -> none  [the longest x12 24.7 us: padded_2(): after = lax.ppermute(first, axis, down)]
    concatenate x4 -> x0, local copies, waits for them, and re-layouts: 47.6 us -> none  [the longest x3 47.5 us: local(): jnp.concatenate([momentum, continuity[None], viscosity[None]], axis=0)]
    pallas_call x0 -> x1, Pallas kernels: none -> 40.7 us  [cycle(): pl.pallas_call(functools.partial(kernel, size), out_shape=(jax.ShapeDtype...]
    reduce_sum x2 -> x0, other arithmetic: 22.1 us -> none  [restrict(): return blocks.mean(axis=(2, 4, 6))]
    reshape x3 -> x0, local copies, waits for them, and re-layouts: 10 us -> none  [the longest x1 7.46 us: restrict(): stacked.reshape(extents[0], extents[1] // 2, 2, extents[2] // 2, 2, exten...]
    slice x21 -> x0, local copies, waits for them, and re-layouts: 8 us -> none  [the longest x9 4.88 us: padded_2(): first = lax.slice_in_dim(array, 0, width, axis=dim)]
    concatenate x27 -> x0, other arithmetic: 6.72 us -> none  [the longest x9 3.38 us: padded_2(): array = jnp.concatenate([before, array, after], axis=dim)]
  transfers between devices with their start and end apart: 48 -> 0, of which waited for: 19 -> 0; matrix products, arithmetic and copies ran while one was open for 10% -> 0% of each run, Pallas kernels for 0% -> 0%
where the time goes in v1:
time: 44 us; the launch traced here: 43.8 us
  Pallas kernels  40.7 us (93%)
  local copies, waits for them, and re-layouts  2.46 us (6%)
  between operations  0.65 us (1%)
    pallas_call x1, Pallas kernels, cycle(): pl.pallas_call(functools.partial(kernel, size), out_shape=(jax.ShapeDtype...  40.7 us
    unnamed x4, local copies, waits for them, and re-layouts  2.46 us

profile of v1, /device:TPU:1, one launch (start us, length us, event | category | flops | bytes accessed | tf_op | source)
XLA Modules:
  0.0 43.8 jit_solution(6185409518497147240)
XLA Ops:
  0.6 40.7 %cycle.1 = (f32[3,8,32,128]{3,2,1,0:T(8,128)}, f32[8,32,128]{2,1,0:T(8,128)}) custom-call(f32[3,8,32,128]{3,2,1,0:T(8,128)} %vel.1, f32[8,32,128]{2,1,0:T(8,128)} %prs.1, f32[8,32,128]{2,1,0:T(8,128)} %vis.1, f32[3,8,32,128]{3,2,1,0:T(8,128)} %frc.1), custom_call_target="tpu_custom_call" | custom-call | tf_op jit(solution)/shard_map/cycle/pallas_call | solution.py:518
  41.4 0.0 copy-start
  41.4 1.8 %copy.8 = f32[3,8,32,128]{3,2,1,0:T(8,128)} copy(f32[3,8,32,128]{3,2,1,0:T(8,128)} %get-tuple-element.4) | data formatting | bytes 786432
  43.2 0.0 copy-done
  43.2 0.7 %copy.9 = f32[8,32,128]{2,1,0:T(8,128)} copy(f32[8,32,128]{2,1,0:T(8,128)S(1)} %copy-done) | data formatting | bytes 262144
Async XLA Ops:
  41.4 1.8 %copy-start = (f32[8,32,128]{2,1,0:T(8,128)S(1)}, f32[8,32,128]{2,1,0:T(8,128)}, u32[]{:S(2)}) copy-start(f32[8,32,128]{2,1,0:T(8,128)} %get-tuple-element.5) | copy-start | bytes 393220

commit v2 on v1

v2 whole, which is shorter than its diff:
```python
import functools
import itertools

import jax
import jax.numpy as jnp
from jax import lax
from jax.experimental import pallas as pl
from jax.experimental.pallas import tpu as pltpu
from jax.sharding import PartitionSpec as P

MESH = pl.DeviceIdType.MESH
F32 = jnp.float32
NX, NZ, NY = 8, 32, 128
CX, CZ = 4, 16
DEEP = 4
HX, HZ = CX + 2 * DEEP, CZ + 2 * DEEP
TOP = 8
OWN = TOP + DEEP
AXES = ("gx", "gy", "gz")
AROUND = [d for d in itertools.product((-1, 0, 1), repeat=3) if any(d)]
FACES = 2 * (3 + 2 + 1 + 3 * 3)


def kernel(
    size, vel, prs, vis, frc, vout, pout,
    u0, u1, u2, u3, u4, visc, force, hvisc, c1, c2, c3, c4,
    wts, scl, diag, rhs, cwts, cscl, tmp, grown, edge, out,
    ysend0, yrecv0, ysend, yrecv,
    vx, vy, vxb, vzb, vyc, vyz, cx, cy, cxb, czb, cyc, cyz,
    send_sem, recv_sem, deep_send, deep_recv, load_sem, store_sem,
):
    at = {axis: lax.axis_index(axis) for axis in AXES}
    has = {}
    for axis in AXES:
        has[axis, 1] = at[axis] < size[axis] - 1
        has[axis, -1] = at[axis] > 0
    lane = lax.broadcasted_iota(jnp.int32, (8, NY), 1)
    row = lax.broadcasted_iota(jnp.int32, (8, NY), 0)
    even = lax.rem(lane, 2) == 0
    couple = lax.div(lane, 2)
    nil = jnp.zeros((8, NY), F32)
    count = [0]
    pending = []

    def roll(value, shift):
        return pltpu.roll(value, shift % NY if isinstance(shift, int) else lax.rem(shift + NY, NY), 1)

    def pick(value, index):
        return jnp.take_along_axis(value, index, axis=1, mode="promise_in_bounds")

    def beside(axis, sign):
        return lax.rem(at[axis] + size[axis] + sign, size[axis])

    def exists(offset, sign=1):
        found = None
        for axis, d in zip(AXES, offset):
            if d:
                one = has[axis, sign * d]
                found = one if found is None else found & one
        return found


    def pair(axis, high_face, low_halo, low_face, high_halo):
        slot = count[0]
        count[0] += 2

        def make(k):
            src, dst, sign = ((high_face, low_halo, 1), (low_face, high_halo, -1))[k]
            return pltpu.make_async_remote_copy(
                src_ref=src, dst_ref=dst,
                send_sem=send_sem.at[slot + k], recv_sem=recv_sem.at[slot + k],
                device_id={axis: beside(axis, sign)}, device_id_type=MESH,
            )

        def each(sign, act):
            @pl.when(has[axis, sign])
            def _():
                act(make(0))

            @pl.when(has[axis, -sign])
            def _():
                act(make(1))

        pending.append(lambda: each(1, lambda c: c.wait_send()))
        return (lambda: each(1, lambda c: c.start())), (lambda: each(-1, lambda c: c.wait_recv()))

    def deep_parts(d, xs, ys, xb, zb, yc, yz):
        dx, dy, dz = d
        if dy == 0 and dz == 0:
            return xs, xb.at[0 if dx > 0 else 1]
        if dy == 0:
            if dz > 0:
                return xs.at[:, :, CZ - DEEP : CZ, :], zb.at[1 - dx, :, :, 0:DEEP, :]
            return xs.at[:, :, 0:DEEP, :], zb.at[1 - dx, :, :, DEEP : 2 * DEEP, :]
        src, side = ys.at[1 if dy > 0 else 0], 0 if dy > 0 else 1
        if dz == 0:
            return src, yc.at[1 - dx, side]
        if dz > 0:
            return src.at[DEEP : 2 * DEEP, :], yz.at[1 - dx, side, 0:DEEP, :]
        return src.at[0:DEEP, :], yz.at[1 - dx, side, DEEP : 2 * DEEP, :]

    def deep_exchange(which, *refs):
        def make(k):
            d = AROUND[k]
            src, dst = deep_parts(d, *refs)
            return pltpu.make_async_remote_copy(
                src_ref=src, dst_ref=dst,
                send_sem=deep_send.at[which, k], recv_sem=deep_recv.at[which, k],
                device_id={axis: beside(axis, s) for axis, s in zip(AXES, d) if s}, device_id_type=MESH,
            )

        def each(sign, act):
            for k, d in enumerate(AROUND):
                @pl.when(exists(d, sign))
                def _():
                    act(make(k))

        pending.append(lambda: each(1, lambda c: c.wait_send()))
        return (lambda: each(1, lambda c: c.start())), (lambda: each(-1, lambda c: c.wait_recv()))

    zs = pl.ds(TOP, NZ)
    planes = pl.ds(1, NX)

    def x_pair(u):
        return pair("gx", u.at[:, NX, zs, :], u.at[:, 0, zs, :], u.at[:, 1, zs, :], u.at[:, NX + 1, zs, :])

    def z_pair(u):
        return pair(
            "gz", u.at[:, planes, TOP + NZ - 1, :], u.at[:, planes, TOP - 1, :],
            u.at[:, planes, TOP, :], u.at[:, planes, TOP + NZ, :],
        )

    def y_pair(sent, received):
        return pair("gy", sent, received.at[0], sent, received.at[1])


    loads = [
        pltpu.make_async_copy(vel, u0.at[0:3, planes, zs, :], load_sem.at[0]),
        pltpu.make_async_copy(prs, u0.at[3, planes, zs, :], load_sem.at[1]),
        pltpu.make_async_copy(vis, visc.at[planes, zs, :], load_sem.at[2]),
        pltpu.make_async_copy(frc, force, load_sem.at[3]),
    ]
    for load in loads:
        load.start()

    barrier = pltpu.get_barrier_semaphore()
    total = jnp.int32(0)
    for axis in AXES:
        for sign in (1, -1):
            @pl.when(has[axis, sign])
            def _():
                pl.semaphore_signal(barrier, inc=1, device_id={axis: beside(axis, sign)}, device_id_type=MESH)
            total = total + has[axis, sign].astype(jnp.int32)
    pl.semaphore_wait(barrier, total)

    first = [
        pair("gx", vel.at[:, NX - 1], u0.at[0:3, 0, zs, :], vel.at[:, 0], u0.at[0:3, NX + 1, zs, :]),
        pair("gx", prs.at[NX - 1], u0.at[3, 0, zs, :], prs.at[0], u0.at[3, NX + 1, zs, :]),
        pair("gx", vis.at[NX - 1], visc.at[0, zs, :], vis.at[0], visc.at[NX + 1, zs, :]),
    ]
    for start, _ in first:
        start()

    def zero(ref):
        ref[...] = jnp.zeros(ref.shape, F32)

    fields = (u0, u1, u2, u4)
    low, high = TOP - 1, TOP + NZ

    def edges(axis, sign, refs):
        @pl.when(jnp.logical_not(has[axis, sign]))
        def _():
            for ref in refs:
                zero(ref)

    edges("gx", -1, [u.at[:, 0, zs, :] for u in fields] + [visc.at[0, zs, :]])
    edges("gx", 1, [u.at[:, NX + 1, zs, :] for u in fields] + [visc.at[NX + 1, zs, :]])
    edges("gz", -1, [u.at[:, planes, low : low + 1, :] for u in fields] + [visc.at[planes, low : low + 1, :]])
    edges("gz", 1, [u.at[:, planes, high : high + 1, :] for u in fields] + [visc.at[planes, high : high + 1, :]])
    edges("gy", -1, [yrecv0.at[0]] + [yrecv.at[s, 0] for s in range(3)])
    edges("gy", 1, [yrecv0.at[1]] + [yrecv.at[s, 1] for s in range(3)])

    for load in loads[:3]:
        load.wait()
    more = [
        z_pair(u0),
        pair(
            "gz", visc.at[planes, TOP + NZ - 1, :], visc.at[planes, TOP - 1, :],
            visc.at[planes, TOP, :], visc.at[planes, TOP + NZ, :],
        ),
    ]
    for start, _ in more:
        start()
    first += more


    def slot_of(k, i, t):
        return (k % 2) * 32 + t * 8 + i

    def put(pack, value, slot):
        return jnp.where(couple == slot, roll(value, 2 * slot + 1), pack)

    def join(from_low, from_high):
        return jnp.where(even, roll(from_high, NY - 1), roll(from_low, 1))

    def ends(joined, slot):
        return roll(joined, NY - 1 - 2 * slot)

    def y_shifts(value, end):
        return jnp.where(lane == 0, end, roll(value, 1)), jnp.where(lane == NY - 1, end, roll(value, NY - 1))

    def first_pack(i, packs):
        a, b, c = packs
        for t in range(4):
            rows = pl.ds(TOP + 8 * t, 8)
            a = put(put(a, u0[0, i + 1, rows, :], slot_of(0, i, t)), u0[1, i + 1, rows, :], slot_of(1, i, t))
            b = put(put(b, u0[2, i + 1, rows, :], slot_of(2, i, t)), u0[3, i + 1, rows, :], slot_of(3, i, t))
            c = put(c, visc[i + 1, rows, :], slot_of(0, i, t))
        return a, b, c

    packs = lax.fori_loop(0, NX, first_pack, (nil, nil, nil), unroll=2)
    for n in range(3):
        ysend0[n] = packs[n]
    more = [y_pair(ysend0, yrecv0)]
    more[0][0]()
    first += more


    doubled = jnp.bitwise_and(2 * lane, NY - 1)
    first_half = lane < NY // 2

    def z_pairs(ref, t):
        return ref[pl.ds(16 * t, 8, stride=2), :] + ref[pl.ds(16 * t + 1, 8, stride=2), :]

    def squeeze(a, b):
        a = a + roll(a, NY - 1)
        b = b + roll(b, NY - 1)
        return jnp.where(first_half, pick(a, doubled), pick(b, doubled))

    group = lax.rem(lax.div(lane, DEEP), 16)

    def deep_slot(f, pp, t):
        return t * 8 + f * 2 + pp

    def deep_pack(xs, ys, nf):
        low_pack, high_pack = nil, nil
        for f in range(nf):
            for pp in range(2):
                for t in range(2):
                    value = xs[f, pp, pl.ds(8 * t, 8), :]
                    s = deep_slot(f, pp, t)
                    low_pack = jnp.where(group == s, roll(value, DEEP * s), low_pack)
                    high_pack = jnp.where(group == s, roll(value, DEEP * s - (NY // 2 - DEEP)), high_pack)
        ys[0], ys[1] = low_pack, high_pack

    def deep_unpack(h, nf, xs, ys, xb, zb, yc, yz):
        for dx in range(3):
            corner = []
            for side in range(2):
                value = yz[dx, side]
                corner.append(jnp.where(row < DEEP, roll(value, -8 * DEEP), value))
            middle = [yc[dx, side] for side in range(2)]
            block = xs if dx == 1 else xb.at[0 if dx == 0 else 1]

            def lay(value, odd, s, sides):
                own = roll(value, DEEP - NY // 2 if odd else DEEP)
                s = s + 16 * odd
                before = roll(sides[0], -DEEP * s)
                after = roll(sides[1], NY // 2 + DEEP - DEEP * s)
                return jnp.where(lane < DEEP, before, jnp.where(lane < NY // 2 + DEEP, own, after))

            for f in range(nf):
                for i in range(CX):
                    pp, odd, x = i // 2, i % 2, dx * CX + i
                    for t in range(2):
                        h[f, x, pl.ds(OWN + 8 * t, 8), :] = lay(
                            block[f, pp, pl.ds(8 * t, 8), :], odd, deep_slot(f, pp, t), middle
                        )
                    both = lay(zb[dx, f, pp], odd, deep_slot(f, pp, 0), corner)
                    h[f, x, pl.ds(TOP, DEEP), :] = both[0:DEEP]
                    h[f, x, pl.ds(OWN + CZ, DEEP), :] = both[DEEP : 2 * DEEP]

    def average(i, _):
        for t in range(4):
            rows = pl.ds(TOP + 8 * t, 8)
            tmp[0, i, pl.ds(8 * t, 8), :] = visc[2 * i + 1, rows, :] + visc[2 * i + 2, rows, :]
        return 0

    lax.fori_loop(0, CX, average, 0, unroll=True)
    for pp in range(2):
        for t in range(2):
            vx[0, pp, pl.ds(8 * t, 8), :] = 0.125 * squeeze(
                z_pairs(tmp.at[0, 2 * pp], t), z_pairs(tmp.at[0, 2 * pp + 1], t)
            )
    deep_pack(vx, vy, 1)
    visc_refs = (vx, vy, vxb, vzb, vyc, vyz)
    flow_refs = (cx, cy, cxb, czb, cyc, cyz)
    for refs in (visc_refs, flow_refs):
        for d in AROUND:
            @pl.when(jnp.logical_not(exists(d, -1)))
            def _():
                zero(deep_parts(d, *refs)[1])

    loads[3].wait()
    for _, wait in first:
        wait()


    def weights(i, _):
        joined = join(yrecv0[0, 2], yrecv0[1, 2])
        for t in range(4):
            r = TOP + 8 * t
            here = visc[i + 1, pl.ds(r, 8), :]
            before, after = y_shifts(here, ends(joined, slot_of(0, i, t)))
            sums = [here + other for other in (
                visc[i, pl.ds(r, 8), :], visc[i + 2, pl.ds(r, 8), :],
                visc[i + 1, pl.ds(r - 1, 8), :], visc[i + 1, pl.ds(r + 1, 8), :],
                before, after,
            )]
            twice = (sums[0] + sums[1]) + (sums[2] + sums[3]) + (sums[4] + sums[5])
            scale = 0.6 / twice
            rows = pl.ds(8 * t, 8)
            for j in range(6):
                wts[j, i, rows, :] = scale * sums[j]
            scl[i, rows, :] = scale
            diag[i, rows, :] = twice * (0.5 / 0.6)
            for k in range(3):
                rhs[k, i, rows, :] = (2.0 * scale) * force[k, i, rows, :]
        return 0

    lax.fori_loop(0, NX, weights, 0, unroll=2)

    def coarse_weights(x, _):
        for t in range(3):
            r = TOP + 8 * t
            here = hvisc[0, x, pl.ds(r, 8), :]
            sums = [here + other for other in (
                hvisc[0, x - 1, pl.ds(r, 8), :], hvisc[0, x + 1, pl.ds(r, 8), :],
                hvisc[0, x, pl.ds(r - 1, 8), :], hvisc[0, x, pl.ds(r + 1, 8), :],
                roll(here, 1), roll(here, NY - 1),
            )]
            twice = (sums[0] + sums[1]) + (sums[2] + sums[3]) + (sums[4] + sums[5])
            scale = jnp.where(here > 0.0, 0.6 / twice, 0.0)
            rows = pl.ds(8 * t, 8)
            for j in range(6):
                cwts[j, x - 1, rows, :] = scale * sums[j]
            cscl[x - 1, rows, :] = scale
        return 0


    def terms(here, around, sides, grad_scale):
        moves, spread = [], None
        for k in range(3):
            parts = [sides[j] * around[j][k] for j in range(6)]
            total = (parts[0] + parts[1]) + (parts[2] + parts[3]) + (parts[4] + parts[5])
            moves.append(total - grad_scale * (around[2 * k + 1][3] - around[2 * k][3]))
            d = around[2 * k + 1][k] - around[2 * k][k]
            spread = d if spread is None else spread + d
        return moves, spread

    def fine_terms(u, end_of, i, t):
        r = TOP + 8 * t
        rows = pl.ds(8 * t, 8)
        here = [u[k, i + 1, pl.ds(r, 8), :] for k in range(4)]
        ys = [y_shifts(here[k], end_of(k, i, t)) for k in range(4)]
        around = (
            [u[k, i, pl.ds(r, 8), :] for k in range(4)],
            [u[k, i + 2, pl.ds(r, 8), :] for k in range(4)],
            [u[k, i + 1, pl.ds(r - 1, 8), :] for k in range(4)],
            [u[k, i + 1, pl.ds(r + 1, 8), :] for k in range(4)],
            [y[0] for y in ys],
            [y[1] for y in ys],
        )
        sides = [wts[j, i, rows, :] for j in range(6)]
        moves, spread = terms(here, around, sides, scl[i, rows, :])
        moves = [m + rhs[k, i, rows, :] for k, m in enumerate(moves)]
        return here, moves, spread

    def fine_update(u, end_of, i, t):
        here, moves, spread = fine_terms(u, end_of, i, t)
        new = [0.4 * here[k] + moves[k] for k in range(3)]
        new.append(here[3] - 0.25 * (visc[i + 1, pl.ds(TOP + 8 * t, 8), :] * spread))
        return new

    def joined_ends(low_pack, high_pack):
        joined = [join(low_pack[n], high_pack[n]) for n in range(2)]
        return lambda k, i, t: ends(joined[k // 2], slot_of(k, i, t))

    def exchange(u, make, sent, received):
        def plane(i, packs):
            packs = list(packs)
            for t in range(4):
                new = make(i, t)
                for k in range(4):
                    u[k, i + 1, pl.ds(TOP + 8 * t, 8), :] = new[k]
                    packs[k // 2] = put(packs[k // 2], new[k], slot_of(k, i, t))
            return tuple(packs)

        packs = plane(NX - 1, plane(0, (nil, nil)))
        x_start, x_wait = x_pair(u)
        x_start()
        packs = lax.fori_loop(1, NX - 1, plane, packs, unroll=2)
        sent[0], sent[1] = packs
        z_start, z_wait = z_pair(u)
        z_start()
        y_start, y_wait = y_pair(sent, received)
        y_start()

        def wait():
            x_wait()
            z_wait()
            y_wait()

        return wait

    ends0 = joined_ends(yrecv0.at[0], yrecv0.at[1])
    wait = exchange(u1, lambda i, t: fine_update(u0, ends0, i, t), ysend.at[0], yrecv.at[0])
    wait()
    visc_start, visc_wait = deep_exchange(0, *visc_refs)
    visc_start()
    ends1 = joined_ends(yrecv.at[0, 0], yrecv.at[0, 1])
    wait = exchange(u2, lambda i, t: fine_update(u1, ends1, i, t), ysend.at[1], yrecv.at[1])
    visc_wait()
    deep_unpack(hvisc, 1, *visc_refs)
    lax.fori_loop(1, HX - 1, coarse_weights, 0, unroll=2)

    def flat(ref, pp, t):
        rows = pl.ds(DEEP + 8 * t, 8)
        a, b = ref[CX + 2 * pp - 1, rows, :], ref[CX + 2 * pp, rows, :]
        return jnp.where(first_half, roll(a, -DEEP), roll(b, NY // 2 - DEEP))

    scales = [[flat(cscl, pp, t) for t in range(2)] for pp in range(2)]
    wait()


    ends2 = joined_ends(yrecv.at[1, 0], yrecv.at[1, 1])

    def restrict(i, _):
        for t in range(4):
            sums = None
            for h in range(2):
                here, moves, spread = fine_terms(u2, ends2, 2 * i + h, t)
                d = diag[2 * i + h, pl.ds(8 * t, 8), :]
                parts = [d * (moves[k] - 0.6 * here[k]) for k in range(3)] + [spread]
                sums = parts if sums is None else [a + b for a, b in zip(sums, parts)]
            for k in range(4):
                tmp[k, i, pl.ds(8 * t, 8), :] = sums[k]
        return 0

    lax.fori_loop(0, CX, restrict, 0)
    for k in range(4):
        for pp in range(2):
            for t in range(2):
                factor = scales[pp][t] if k < 3 else -0.03125 * vx[0, pp, pl.ds(8 * t, 8), :]
                cx[k, pp, pl.ds(8 * t, 8), :] = factor * squeeze(
                    z_pairs(tmp.at[k, 2 * pp], t), z_pairs(tmp.at[k, 2 * pp + 1], t)
                )
    deep_pack(cx, cy, 4)
    flow_start, flow_wait = deep_exchange(1, *flow_refs)
    flow_start()
    flow_wait()
    deep_unpack(c1, 4, *flow_refs)

    def coarse_sweep(old, new, start, stop):
        def plane(x, _):
            for t in range(3):
                r = TOP + 8 * t
                rows = pl.ds(8 * t, 8)
                here = [old[k, x, pl.ds(r, 8), :] for k in range(4)]
                around = (
                    [old[k, x - 1, pl.ds(r, 8), :] for k in range(4)],
                    [old[k, x + 1, pl.ds(r, 8), :] for k in range(4)],
                    [old[k, x, pl.ds(r - 1, 8), :] for k in range(4)],
                    [old[k, x, pl.ds(r + 1, 8), :] for k in range(4)],
                    [roll(h, 1) for h in here],
                    [roll(h, NY - 1) for h in here],
                )
                sides = [cwts[j, x - 1, rows, :] for j in range(6)]
                moves, spread = terms(here, around, sides, 2.0 * cscl[x - 1, rows, :])
                source = [c1[k, x, pl.ds(r, 8), :] for k in range(4)]
                for k in range(3):
                    new[k, x, pl.ds(r, 8), :] = 0.4 * here[k] + (moves[k] + source[k])
                new[3, x, pl.ds(r, 8), :] = here[3] + (
                    source[3] - 0.125 * (hvisc[0, x, pl.ds(r, 8), :] * spread)
                )
            return 0

        lax.fori_loop(start, stop, plane, 0, unroll=2)

    coarse_sweep(c1, c2, 1, HX - 1)
    coarse_sweep(c2, c3, 2, HX - 2)
    coarse_sweep(c3, c4, 3, HX - 3)


    spread_out = DEEP + couple
    past_ends = jnp.where(lane < NY // 2, DEEP - 1, NY // 2 + DEEP)

    def prolong(x, _):
        for k in range(4):
            for t in range(2):
                value = pick(c4[k, x + 3, pl.ds(OWN + 8 * t, 8), :], spread_out)
                grown[k, x, pl.ds(TOP + 16 * t, 8, stride=2), :] = value
                grown[k, x, pl.ds(TOP + 16 * t + 1, 8, stride=2), :] = value
        return 0

    def prolong_sides(x, _):
        for k in range(4):
            above = pick(c4[k, x + 3, pl.ds(TOP, 8), :], spread_out)
            grown[k, x, TOP - 1 : TOP, :] = above[DEEP - 1 : DEEP]
            below = pick(c4[k, x + 3, pl.ds(OWN + CZ - DEEP, 8), :], spread_out)
            grown[k, x, TOP + NZ : TOP + NZ + 1, :] = below[DEEP : DEEP + 1]
            for t in range(2):
                value = pick(c4[k, x + 3, pl.ds(OWN + 8 * t, 8), :], past_ends)
                edge[k, x - 1, pl.ds(16 * t, 8, stride=2), :] = value
                edge[k, x - 1, pl.ds(16 * t + 1, 8, stride=2), :] = value
        return 0

    lax.fori_loop(0, CX + 2, prolong, 0, unroll=2)
    lax.fori_loop(1, CX + 1, prolong_sides, 0, unroll=2)

    def correct(i, _):
        half = lax.div(i + 1, 2)
        for k in range(4):
            for t in range(4):
                rows = pl.ds(TOP + 8 * t, 8)
                u3[k, i, rows, :] = u2[k, i, rows, :] + grown[k, half, rows, :]
            for r in (TOP - 1, TOP + NZ):
                u3[k, i, r : r + 1, :] = u2[k, i, r : r + 1, :] + grown[k, half, r : r + 1, :]
        return 0

    lax.fori_loop(1, NX + 1, correct, 0, unroll=2)
    for i, x in ((0, 0), (NX + 1, CX + 1)):
        for k in range(4):
            for t in range(4):
                rows = pl.ds(TOP + 8 * t, 8)
                u3[k, i, rows, :] = u2[k, i, rows, :] + grown[k, x, rows, :]

    def ends3(k, i, t):
        return ends2(k, i, t) + edge[k, lax.div(i, 2) if not isinstance(i, int) else i // 2, pl.ds(8 * t, 8), :]


    wait = exchange(u4, lambda i, t: fine_update(u3, ends3, i, t), ysend.at[2], yrecv.at[2])
    wait()
    ends4 = joined_ends(yrecv.at[2, 0], yrecv.at[2, 1])

    def stores(i):
        return (
            pltpu.make_async_copy(out.at[0:3, i], vout.at[:, i], store_sem.at[0, i]),
            pltpu.make_async_copy(out.at[3, i], pout.at[i], store_sem.at[1, i]),
        )

    def last(i, _):
        for t in range(4):
            new = fine_update(u4, ends4, i, t)
            for k in range(4):
                out[k, i, pl.ds(8 * t, 8), :] = new[k]
        for store in stores(i):
            store.start()
        return 0

    lax.fori_loop(0, NX, last, 0, unroll=2)
    for i in range(NX):
        for store in stores(i):
            store.wait()
    for drain in pending:
        drain()


def cycle(size, velocity, pressure, viscosity, body_force):
    field = pltpu.VMEM((4, NX + 2, NZ + 16, NY), F32)
    small = pltpu.VMEM((4, HX, HZ + 16, NY), F32)
    anywhere = pl.BlockSpec(memory_space=pl.ANY)

    def deep_buffers(nf):
        return [
            pltpu.VMEM((nf, 2, CZ, NY), F32),
            pltpu.VMEM((2, 8, NY), F32),
            pltpu.VMEM((2, nf, 2, CZ, NY), F32),
            pltpu.VMEM((3, nf, 2, 8, NY), F32),
            pltpu.VMEM((3, 2, 8, NY), F32),
            pltpu.VMEM((3, 2, 8, NY), F32),
        ]

    out = pl.pallas_call(
        functools.partial(kernel, size),
        out_shape=(
            jax.ShapeDtypeStruct((3, NX, NZ, NY), F32),
            jax.ShapeDtypeStruct((NX, NZ, NY), F32),
        ),
        in_specs=[anywhere] * 4,
        out_specs=(anywhere, anywhere),
        scratch_shapes=[
            field, field, field, field, field,
            pltpu.VMEM((NX + 2, NZ + 16, NY), F32),
            pltpu.VMEM((3, NX, NZ, NY), F32),
            pltpu.VMEM((1, HX, HZ + 16, NY), F32),
            small, small, small, small,
            pltpu.VMEM((6, NX, NZ, NY), F32),
            pltpu.VMEM((NX, NZ, NY), F32),
            pltpu.VMEM((NX, NZ, NY), F32),
            pltpu.VMEM((3, NX, NZ, NY), F32),
            pltpu.VMEM((6, HX - 2, HZ, NY), F32),
            pltpu.VMEM((HX - 2, HZ, NY), F32),
            pltpu.VMEM((4, CX, NZ, NY), F32),
            pltpu.VMEM((4, CX + 2, NZ + 16, NY), F32),
            pltpu.VMEM((4, CX, NZ, NY), F32),
            pltpu.VMEM((4, NX, NZ, NY), F32),
            pltpu.VMEM((3, 8, NY), F32),
            pltpu.VMEM((2, 3, 8, NY), F32),
            pltpu.VMEM((3, 2, 8, NY), F32),
            pltpu.VMEM((3, 2, 2, 8, NY), F32),
            *deep_buffers(1),
            *deep_buffers(4),
            pltpu.SemaphoreType.DMA((FACES,)),
            pltpu.SemaphoreType.DMA((FACES,)),
            pltpu.SemaphoreType.DMA((2, len(AROUND))),
            pltpu.SemaphoreType.DMA((2, len(AROUND))),
            pltpu.SemaphoreType.DMA((4,)),
            pltpu.SemaphoreType.DMA((2, NX)),
        ],
        compiler_params=pltpu.CompilerParams(collective_id=0, has_side_effects=True),
        name="cycle",
    )(velocity, pressure, viscosity, body_force)
    return out[0], out[1]


def solution(mesh):
    return jax.shard_map(
        functools.partial(cycle, dict(mesh.shape)),
        mesh=mesh,
        in_specs=(
            P(None, "gx", "gz", "gy"),
            P("gx", "gz", "gy"),
            P("gx", "gz", "gy"),
            P(None, "gx", "gz", "gy"),
        ),
        out_specs=(P(None, "gx", "gz", "gy"), P("gx", "gz", "gy")),
        check_vma=False,
    )
```

time: 44 us -> 35.5 us (0.81)
  Pallas kernels: 40.7 us -> 32.3 us
    pallas_call x1, Pallas kernels: 40.7 us -> 32.3 us  [cycle(): pl.pallas_call(functools.partial(kernel, size), out_shape=(jax.ShapeDtype...]
where the time goes in v2:
time: 35.5 us; the launch traced here: 35.4 us
  Pallas kernels  32.3 us (91%)
  local copies, waits for them, and re-layouts  2.46 us (7%)
  between operations  0.65 us (2%)
    pallas_call x1, Pallas kernels, cycle(): pl.pallas_call(functools.partial(kernel, size), out_shape=(jax.ShapeDtype...  32.3 us
    unnamed x4, local copies, waits for them, and re-layouts  2.46 us

profile of v2, /device:TPU:1, one launch (start us, length us, event | category | flops | bytes accessed | tf_op | source)
XLA Modules:
  0.0 35.4 jit_solution(11714504425831558889)
XLA Ops:
  0.6 32.3 %cycle.1 = (f32[3,8,32,128]{3,2,1,0:T(8,128)}, f32[8,32,128]{2,1,0:T(8,128)}) custom-call(f32[3,8,32,128]{3,2,1,0:T(8,128)} %vel.1, f32[8,32,128]{2,1,0:T(8,128)} %prs.1, f32[8,32,128]{2,1,0:T(8,128)} %vis.1, f32[3,8,32,128]{3,2,1,0:T(8,128)} %frc.1), custom_call_target="tpu_custom_call" | custom-call | tf_op jit(solution)/shard_map/cycle/pallas_call | solution.py:584
  32.9 0.0 copy-start
  33.0 1.8 %copy.8 = f32[3,8,32,128]{3,2,1,0:T(8,128)} copy(f32[3,8,32,128]{3,2,1,0:T(8,128)} %get-tuple-element.4) | data formatting | bytes 786432
  34.8 0.0 copy-done
  34.8 0.7 %copy.9 = f32[8,32,128]{2,1,0:T(8,128)} copy(f32[8,32,128]{2,1,0:T(8,128)S(1)} %copy-done) | data formatting | bytes 262144
Async XLA Ops:
  32.9 1.8 %copy-start = (f32[8,32,128]{2,1,0:T(8,128)S(1)}, f32[8,32,128]{2,1,0:T(8,128)}, u32[]{:S(2)}) copy-start(f32[8,32,128]{2,1,0:T(8,128)} %get-tuple-element.5) | copy-start | bytes 393220

commit v3 on v2

--- a/solution.py
+++ b/solution.py
@@ -17,14 +17,17 @@
 TOP = 8
 OWN = TOP + DEEP
 AXES = ("gx", "gy", "gz")
-AROUND = [d for d in itertools.product((-1, 0, 1), repeat=3) if any(d)]
+AROUND = sorted(
+    (d for d in itertools.product((-1, 0, 1), repeat=3) if any(d)),
+    key=lambda d: (d[1:] != (0, 0), -sum(map(abs, d))),
+)
 FACES = 2 * (3 + 2 + 1 + 3 * 3)
 
 
 def kernel(
     size, vel, prs, vis, frc, vout, pout,
     u0, u1, u2, u3, u4, visc, force, hvisc, c1, c2, c3, c4,
-    wts, scl, diag, rhs, cwts, cscl, tmp, grown, edge, out,
+    wts, scl, diag, rhs, cwts, cscl, tmp, grown, gprev, gnext, yprev, ynext, out,
     ysend0, yrecv0, ysend, yrecv,
     vx, vy, vxb, vzb, vyc, vyz, cx, cy, cxb, czb, cyc, cyz,
     send_sem, recv_sem, deep_send, deep_recv, load_sem, store_sem,
@@ -42,6 +45,10 @@
     count = [0]
     pending = []
 
+    def drain(keep=0):
+        while len(pending) > keep:
+            pending.pop(0)()
+
     def roll(value, shift):
         return pltpu.roll(value, shift % NY if isinstance(shift, int) else lax.rem(shift + NY, NY), 1)
 
@@ -92,12 +99,12 @@
             if dz > 0:
                 return xs.at[:, :, CZ - DEEP : CZ, :], zb.at[1 - dx, :, :, 0:DEEP, :]
             return xs.at[:, :, 0:DEEP, :], zb.at[1 - dx, :, :, DEEP : 2 * DEEP, :]
-        src, side = ys.at[1 if dy > 0 else 0], 0 if dy > 0 else 1
+        side = 0 if dy > 0 else 1
         if dz == 0:
-            return src, yc.at[1 - dx, side]
+            return ys, yc.at[1 - dx, side]
         if dz > 0:
-            return src.at[DEEP : 2 * DEEP, :], yz.at[1 - dx, side, 0:DEEP, :]
-        return src.at[0:DEEP, :], yz.at[1 - dx, side, DEEP : 2 * DEEP, :]
+            return ys.at[:, DEEP : 2 * DEEP, :], yz.at[1 - dx, side, :, 0:DEEP, :]
+        return ys.at[:, 0:DEEP, :], yz.at[1 - dx, side, :, DEEP : 2 * DEEP, :]
 
     def deep_exchange(which, *refs):
         def make(k):
@@ -206,8 +213,21 @@
     def ends(joined, slot):
         return roll(joined, NY - 1 - 2 * slot)
 
-    def y_shifts(value, end):
-        return jnp.where(lane == 0, end, roll(value, 1)), jnp.where(lane == NY - 1, end, roll(value, NY - 1))
+    def y_shifts(k, i, t, end):
+        rows = pl.ds(8 * t, 8)
+        return jnp.where(lane == 0, end, yprev[k, i, rows, :]), jnp.where(lane == NY - 1, end, ynext[k, i, rows, :])
+
+    def rotate(u, more=None):
+        def plane(i, _):
+            for t in range(4):
+                for k in range(4 if more is None else 5):
+                    rows = pl.ds(TOP + 8 * t, 8)
+                    value = u[k, i + 1, rows, :] if k < 4 else more[i + 1, rows, :]
+                    yprev[k, i, pl.ds(8 * t, 8), :] = roll(value, 1)
+                    ynext[k, i, pl.ds(8 * t, 8), :] = roll(value, NY - 1)
+            return 0
+
+        lax.fori_loop(0, NX, plane, 0, unroll=2)
 
     def first_pack(i, packs):
         a, b, c = packs
@@ -237,46 +257,44 @@
         b = b + roll(b, NY - 1)
         return jnp.where(first_half, pick(a, doubled), pick(b, doubled))
 
-    group = lax.rem(lax.div(lane, DEEP), 16)
+    octet, fore = lax.div(lane, 2 * DEEP), lax.rem(lane, 2 * DEEP) < DEEP
 
     def deep_slot(f, pp, t):
-        return t * 8 + f * 2 + pp
+        return (f % 2) * 4 + t * 2 + pp
 
     def deep_pack(xs, ys, nf):
-        low_pack, high_pack = nil, nil
-        for f in range(nf):
-            for pp in range(2):
-                for t in range(2):
-                    value = xs[f, pp, pl.ds(8 * t, 8), :]
-                    s = deep_slot(f, pp, t)
-                    low_pack = jnp.where(group == s, roll(value, DEEP * s), low_pack)
-                    high_pack = jnp.where(group == s, roll(value, DEEP * s - (NY // 2 - DEEP)), high_pack)
-        ys[0], ys[1] = low_pack, high_pack
+        for n in range((nf + 1) // 2):
+            pack = nil
+            for f in range(2 * n, min(2 * n + 2, nf)):
+                for pp in range(2):
+                    for t in range(2):
+                        s = deep_slot(f, pp, t)
+                        first = fore & (lax.rem(octet, 8) == s)
+                        last = jnp.logical_not(fore) & (lax.rem(octet + 1, 8) == s)
+                        pack = jnp.where(first | last, roll(xs[f, pp, pl.ds(8 * t, 8), :], 8 * s), pack)
+            ys[n] = pack
 
     def deep_unpack(h, nf, xs, ys, xb, zb, yc, yz):
         for dx in range(3):
-            corner = []
-            for side in range(2):
-                value = yz[dx, side]
-                corner.append(jnp.where(row < DEEP, roll(value, -8 * DEEP), value))
-            middle = [yc[dx, side] for side in range(2)]
+            middle, corner = [], []
+            for n in range((nf + 1) // 2):
+                middle.append(jnp.where(fore, yc[dx, 1, n], yc[dx, 0, n]))
+                value = jnp.where(fore, yz[dx, 1, n], yz[dx, 0, n])
+                corner.append(jnp.where(row < DEEP, roll(value, -4 * DEEP), value))
             block = xs if dx == 1 else xb.at[0 if dx == 0 else 1]
 
             def lay(value, odd, s, sides):
-                own = roll(value, DEEP - NY // 2 if odd else DEEP)
-                s = s + 16 * odd
-                before = roll(sides[0], -DEEP * s)
-                after = roll(sides[1], NY // 2 + DEEP - DEEP * s)
-                return jnp.where(lane < DEEP, before, jnp.where(lane < NY // 2 + DEEP, own, after))
+                own = roll(value, NY // 2) if odd else value
+                return jnp.where(first_half, own, roll(sides, NY // 2 - 8 * (s + 8 * odd)))
 
             for f in range(nf):
                 for i in range(CX):
                     pp, odd, x = i // 2, i % 2, dx * CX + i
                     for t in range(2):
                         h[f, x, pl.ds(OWN + 8 * t, 8), :] = lay(
-                            block[f, pp, pl.ds(8 * t, 8), :], odd, deep_slot(f, pp, t), middle
+                            block[f, pp, pl.ds(8 * t, 8), :], odd, deep_slot(f, pp, t), middle[f // 2]
                         )
-                    both = lay(zb[dx, f, pp], odd, deep_slot(f, pp, 0), corner)
+                    both = lay(zb[dx, f, pp], odd, deep_slot(f, pp, 0), corner[f // 2])
                     h[f, x, pl.ds(TOP, DEEP), :] = both[0:DEEP]
                     h[f, x, pl.ds(OWN + CZ, DEEP), :] = both[DEEP : 2 * DEEP]
 
@@ -301,6 +319,7 @@
             def _():
                 zero(deep_parts(d, *refs)[1])
 
+    rotate(u0, visc)
     loads[3].wait()
     for _, wait in first:
         wait()
@@ -311,7 +330,7 @@
         for t in range(4):
             r = TOP + 8 * t
             here = visc[i + 1, pl.ds(r, 8), :]
-            before, after = y_shifts(here, ends(joined, slot_of(0, i, t)))
+            before, after = y_shifts(4, i, t, ends(joined, slot_of(0, i, t)))
             sums = [here + other for other in (
                 visc[i, pl.ds(r, 8), :], visc[i + 2, pl.ds(r, 8), :],
                 visc[i + 1, pl.ds(r - 1, 8), :], visc[i + 1, pl.ds(r + 1, 8), :],
@@ -358,11 +377,11 @@
             spread = d if spread is None else spread + d
         return moves, spread
 
-    def fine_terms(u, end_of, i, t):
+    def fine_terms(u, y_of, i, t):
         r = TOP + 8 * t
         rows = pl.ds(8 * t, 8)
         here = [u[k, i + 1, pl.ds(r, 8), :] for k in range(4)]
-        ys = [y_shifts(here[k], end_of(k, i, t)) for k in range(4)]
+        ys = [y_of(k, i, t) for k in range(4)]
         around = (
             [u[k, i, pl.ds(r, 8), :] for k in range(4)],
             [u[k, i + 2, pl.ds(r, 8), :] for k in range(4)],
@@ -376,15 +395,15 @@
         moves = [m + rhs[k, i, rows, :] for k, m in enumerate(moves)]
         return here, moves, spread
 
-    def fine_update(u, end_of, i, t):
-        here, moves, spread = fine_terms(u, end_of, i, t)
+    def fine_update(u, y_of, i, t):
+        here, moves, spread = fine_terms(u, y_of, i, t)
         new = [0.4 * here[k] + moves[k] for k in range(3)]
         new.append(here[3] - 0.25 * (visc[i + 1, pl.ds(TOP + 8 * t, 8), :] * spread))
         return new
 
     def joined_ends(low_pack, high_pack):
         joined = [join(low_pack[n], high_pack[n]) for n in range(2)]
-        return lambda k, i, t: ends(joined[k // 2], slot_of(k, i, t))
+        return lambda k, i, t: y_shifts(k, i, t, ends(joined[k // 2], slot_of(k, i, t)))
 
     def exchange(u, make, sent, received):
         def plane(i, packs):
@@ -415,11 +434,14 @@
 
     ends0 = joined_ends(yrecv0.at[0], yrecv0.at[1])
     wait = exchange(u1, lambda i, t: fine_update(u0, ends0, i, t), ysend.at[0], yrecv.at[0])
+    rotate(u1)
+    drain(3)
     wait()
     visc_start, visc_wait = deep_exchange(0, *visc_refs)
     visc_start()
     ends1 = joined_ends(yrecv.at[0, 0], yrecv.at[0, 1])
     wait = exchange(u2, lambda i, t: fine_update(u1, ends1, i, t), ysend.at[1], yrecv.at[1])
+    rotate(u2)
     visc_wait()
     deep_unpack(hvisc, 1, *visc_refs)
     lax.fori_loop(1, HX - 1, coarse_weights, 0, unroll=2)
@@ -427,7 +449,7 @@
     def flat(ref, pp, t):
         rows = pl.ds(DEEP + 8 * t, 8)
         a, b = ref[CX + 2 * pp - 1, rows, :], ref[CX + 2 * pp, rows, :]
-        return jnp.where(first_half, roll(a, -DEEP), roll(b, NY // 2 - DEEP))
+        return jnp.where(first_half, a, roll(b, NY // 2))
 
     scales = [[flat(cscl, pp, t) for t in range(2)] for pp in range(2)]
     wait()
@@ -458,6 +480,16 @@
     deep_pack(cx, cy, 4)
     flow_start, flow_wait = deep_exchange(1, *flow_refs)
     flow_start()
+
+    def insert_ends(i, _):
+        for t in range(4):
+            rows = pl.ds(8 * t, 8)
+            for k in range(4):
+                yprev[k, i, rows, :], ynext[k, i, rows, :] = ends2(k, i, t)
+        return 0
+
+    lax.fori_loop(0, NX, insert_ends, 0, unroll=2)
+    drain(1)
     flow_wait()
     deep_unpack(c1, 4, *flow_refs)
 
@@ -492,27 +524,28 @@
     coarse_sweep(c3, c4, 3, HX - 3)
 
 
-    spread_out = DEEP + couple
-    past_ends = jnp.where(lane < NY // 2, DEEP - 1, NY // 2 + DEEP)
+    parents = (couple, jnp.where(lane == 0, NY - 1, lax.div(lane + 1, 2) - 1), lax.div(lane + 1, 2))
+
+    def widen(ref, start, value):
+        ref[pl.ds(start, 8, stride=2), :] = value
+        ref[pl.ds(start + 1, 8, stride=2), :] = value
 
     def prolong(x, _):
         for k in range(4):
             for t in range(2):
-                value = pick(c4[k, x + 3, pl.ds(OWN + 8 * t, 8), :], spread_out)
-                grown[k, x, pl.ds(TOP + 16 * t, 8, stride=2), :] = value
-                grown[k, x, pl.ds(TOP + 16 * t + 1, 8, stride=2), :] = value
+                widen(grown.at[k, x], TOP + 16 * t, pick(c4[k, x + 3, pl.ds(OWN + 8 * t, 8), :], parents[0]))
         return 0
 
     def prolong_sides(x, _):
         for k in range(4):
-            above = pick(c4[k, x + 3, pl.ds(TOP, 8), :], spread_out)
+            above = pick(c4[k, x + 3, pl.ds(TOP, 8), :], parents[0])
             grown[k, x, TOP - 1 : TOP, :] = above[DEEP - 1 : DEEP]
-            below = pick(c4[k, x + 3, pl.ds(OWN + CZ - DEEP, 8), :], spread_out)
+            below = pick(c4[k, x + 3, pl.ds(OWN + CZ - DEEP, 8), :], parents[0])
             grown[k, x, TOP + NZ : TOP + NZ + 1, :] = below[DEEP : DEEP + 1]
             for t in range(2):
-                value = pick(c4[k, x + 3, pl.ds(OWN + 8 * t, 8), :], past_ends)
-                edge[k, x - 1, pl.ds(16 * t, 8, stride=2), :] = value
-                edge[k, x - 1, pl.ds(16 * t + 1, 8, stride=2), :] = value
+                value = c4[k, x + 3, pl.ds(OWN + 8 * t, 8), :]
+                widen(gprev.at[k, x - 1], 16 * t, pick(value, parents[1]))
+                widen(gnext.at[k, x - 1], 16 * t, pick(value, parents[2]))
         return 0
 
     lax.fori_loop(0, CX + 2, prolong, 0, unroll=2)
@@ -536,10 +569,14 @@
                 u3[k, i, rows, :] = u2[k, i, rows, :] + grown[k, x, rows, :]
 
     def ends3(k, i, t):
-        return ends2(k, i, t) + edge[k, lax.div(i, 2) if not isinstance(i, int) else i // 2, pl.ds(8 * t, 8), :]
+        rows = pl.ds(8 * t, 8)
+        half = i // 2 if isinstance(i, int) else lax.div(i, 2)
+        return yprev[k, i, rows, :] + gprev[k, half, rows, :], ynext[k, i, rows, :] + gnext[k, half, rows, :]
 
 
     wait = exchange(u4, lambda i, t: fine_update(u3, ends3, i, t), ysend.at[2], yrecv.at[2])
+    rotate(u4)
+    drain(3)
     wait()
     ends4 = joined_ends(yrecv.at[2, 0], yrecv.at[2, 1])
 
@@ -562,8 +599,7 @@
     for i in range(NX):
         for store in stores(i):
             store.wait()
-    for drain in pending:
-        drain()
+    drain()
 
 
 def cycle(size, velocity, pressure, viscosity, body_force):
@@ -574,11 +610,11 @@
     def deep_buffers(nf):
         return [
             pltpu.VMEM((nf, 2, CZ, NY), F32),
-            pltpu.VMEM((2, 8, NY), F32),
+            pltpu.VMEM(((nf + 1) // 2, 8, NY), F32),
             pltpu.VMEM((2, nf, 2, CZ, NY), F32),
             pltpu.VMEM((3, nf, 2, 8, NY), F32),
-            pltpu.VMEM((3, 2, 8, NY), F32),
-            pltpu.VMEM((3, 2, 8, NY), F32),
+            pltpu.VMEM((3, 2, (nf + 1) // 2, 8, NY), F32),
+            pltpu.VMEM((3, 2, (nf + 1) // 2, 8, NY), F32),
         ]
 
     out = pl.pallas_call(
@@ -604,6 +640,9 @@
             pltpu.VMEM((4, CX, NZ, NY), F32),
             pltpu.VMEM((4, CX + 2, NZ + 16, NY), F32),
             pltpu.VMEM((4, CX, NZ, NY), F32),
+            pltpu.VMEM((4, CX, NZ, NY), F32),
+            pltpu.VMEM((5, NX, NZ, NY), F32),
+            pltpu.VMEM((5, NX, NZ, NY), F32),
             pltpu.VMEM((4, NX, NZ, NY), F32),
             pltpu.VMEM((3, 8, NY), F32),
             pltpu.VMEM((2, 3, 8, NY), F32),

time: 35.5 us -> 34.6 us (0.975)
  Pallas kernels: 32.3 us -> 31.3 us
    pallas_call x1, Pallas kernels: 32.3 us -> 31.3 us  [cycle(): pl.pallas_call(functools.partial(kernel, size), out_shape=(jax.ShapeDtype...]
where the time goes in v3:
time: 34.6 us; the launch traced here: 34.4 us
  Pallas kernels  31.3 us (90%)
  local copies, waits for them, and re-layouts  2.46 us (7%)
  between operations  0.65 us (2%)
    pallas_call x1, Pallas kernels, cycle(): pl.pallas_call(functools.partial(kernel, size), out_shape=(jax.ShapeDtype...  31.3 us
    unnamed x4, local copies, waits for them, and re-layouts  2.46 us

profile of v3, /device:TPU:1, one launch (start us, length us, event | category | flops | bytes accessed | tf_op | source)
XLA Modules:
  0.0 34.4 jit_solution(17713918586116011049)
XLA Ops:
  0.6 31.3 %cycle.1 = (f32[3,8,32,128]{3,2,1,0:T(8,128)}, f32[8,32,128]{2,1,0:T(8,128)}) custom-call(f32[3,8,32,128]{3,2,1,0:T(8,128)} %vel.1, f32[8,32,128]{2,1,0:T(8,128)} %prs.1, f32[8,32,128]{2,1,0:T(8,128)} %vis.1, f32[3,8,32,128]{3,2,1,0:T(8,128)} %frc.1), custom_call_target="tpu_custom_call" | custom-call | tf_op jit(solution)/shard_map/cycle/pallas_call | solution.py:620
  32.0 0.0 copy-start
  32.0 1.8 %copy.8 = f32[3,8,32,128]{3,2,1,0:T(8,128)} copy(f32[3,8,32,128]{3,2,1,0:T(8,128)} %get-tuple-element.4) | data formatting | bytes 786432
  33.8 0.0 copy-done
  33.8 0.7 %copy.9 = f32[8,32,128]{2,1,0:T(8,128)} copy(f32[8,32,128]{2,1,0:T(8,128)S(1)} %copy-done) | data formatting | bytes 262144
Async XLA Ops:
  32.0 1.8 %copy-start = (f32[8,32,128]{2,1,0:T(8,128)S(1)}, f32[8,32,128]{2,1,0:T(8,128)}, u32[]{:S(2)}) copy-start(f32[8,32,128]{2,1,0:T(8,128)} %get-tuple-element.5) | copy-start | bytes 393220

commit v4 on v3

--- a/solution.py
+++ b/solution.py
@@ -21,7 +21,7 @@
     (d for d in itertools.product((-1, 0, 1), repeat=3) if any(d)),
     key=lambda d: (d[1:] != (0, 0), -sum(map(abs, d))),
 )
-FACES = 2 * (3 + 2 + 1 + 3 * 3)
+FACES = 2 * (2 + 2 + 1 + 3 * 3)
 
 
 def kernel(
@@ -50,7 +50,7 @@
             pending.pop(0)()
 
     def roll(value, shift):
-        return pltpu.roll(value, shift % NY if isinstance(shift, int) else lax.rem(shift + NY, NY), 1)
+        return pltpu.roll(value, shift % NY if isinstance(shift, int) else shift, 1)
 
     def pick(value, index):
         return jnp.take_along_axis(value, index, axis=1, mode="promise_in_bounds")
@@ -116,14 +116,18 @@
                 device_id={axis: beside(axis, s) for axis, s in zip(AXES, d) if s}, device_id_type=MESH,
             )
 
-        def each(sign, act):
+        def each(sign, act, hops=(1, 2, 3)):
             for k, d in enumerate(AROUND):
-                @pl.when(exists(d, sign))
-                def _():
-                    act(make(k))
+                if sum(map(abs, d)) in hops:
+                    @pl.when(exists(d, sign))
+                    def _():
+                        act(make(k))
+
+        def start(*hops):
+            each(1, lambda c: c.start(), hops)
 
         pending.append(lambda: each(1, lambda c: c.wait_send()))
-        return (lambda: each(1, lambda c: c.start())), (lambda: each(-1, lambda c: c.wait_recv()))
+        return start, (lambda: each(-1, lambda c: c.wait_recv()))
 
     zs = pl.ds(TOP, NZ)
     planes = pl.ds(1, NX)
@@ -158,15 +162,6 @@
             def _():
                 pl.semaphore_signal(barrier, inc=1, device_id={axis: beside(axis, sign)}, device_id_type=MESH)
             total = total + has[axis, sign].astype(jnp.int32)
-    pl.semaphore_wait(barrier, total)
-
-    first = [
-        pair("gx", vel.at[:, NX - 1], u0.at[0:3, 0, zs, :], vel.at[:, 0], u0.at[0:3, NX + 1, zs, :]),
-        pair("gx", prs.at[NX - 1], u0.at[3, 0, zs, :], prs.at[0], u0.at[3, NX + 1, zs, :]),
-        pair("gx", vis.at[NX - 1], visc.at[0, zs, :], vis.at[0], visc.at[NX + 1, zs, :]),
-    ]
-    for start, _ in first:
-        start()
 
     def zero(ref):
         ref[...] = jnp.zeros(ref.shape, F32)
@@ -189,16 +184,6 @@
 
     for load in loads[:3]:
         load.wait()
-    more = [
-        z_pair(u0),
-        pair(
-            "gz", visc.at[planes, TOP + NZ - 1, :], visc.at[planes, TOP - 1, :],
-            visc.at[planes, TOP, :], visc.at[planes, TOP + NZ, :],
-        ),
-    ]
-    for start, _ in more:
-        start()
-    first += more
 
 
     def slot_of(k, i, t):
@@ -241,9 +226,20 @@
     packs = lax.fori_loop(0, NX, first_pack, (nil, nil, nil), unroll=2)
     for n in range(3):
         ysend0[n] = packs[n]
-    more = [y_pair(ysend0, yrecv0)]
-    more[0][0]()
-    first += more
+
+    pl.semaphore_wait(barrier, total)
+    first = [
+        x_pair(u0),
+        pair("gx", visc.at[NX, zs, :], visc.at[0, zs, :], visc.at[1, zs, :], visc.at[NX + 1, zs, :]),
+        y_pair(ysend0, yrecv0),
+        z_pair(u0),
+        pair(
+            "gz", visc.at[planes, TOP + NZ - 1, :], visc.at[planes, TOP - 1, :],
+            visc.at[planes, TOP, :], visc.at[planes, TOP + NZ, :],
+        ),
+    ]
+    for start, _ in first:
+        start()
 
 
     doubled = jnp.bitwise_and(2 * lane, NY - 1)
@@ -436,9 +432,10 @@
     wait = exchange(u1, lambda i, t: fine_update(u0, ends0, i, t), ysend.at[0], yrecv.at[0])
     rotate(u1)
     drain(3)
+    visc_start, visc_wait = deep_exchange(0, *visc_refs)
+    visc_start(1, 2)
     wait()
-    visc_start, visc_wait = deep_exchange(0, *visc_refs)
-    visc_start()
+    visc_start(3)
     ends1 = joined_ends(yrecv.at[0, 0], yrecv.at[0, 1])
     wait = exchange(u2, lambda i, t: fine_update(u1, ends1, i, t), ysend.at[1], yrecv.at[1])
     rotate(u2)
@@ -479,7 +476,7 @@
                 )
     deep_pack(cx, cy, 4)
     flow_start, flow_wait = deep_exchange(1, *flow_refs)
-    flow_start()
+    flow_start(1, 2, 3)
 
     def insert_ends(i, _):
         for t in range(4):
@@ -576,14 +573,15 @@
 
     wait = exchange(u4, lambda i, t: fine_update(u3, ends3, i, t), ysend.at[2], yrecv.at[2])
     rotate(u4)
-    drain(3)
+    drain()
     wait()
     ends4 = joined_ends(yrecv.at[2, 0], yrecv.at[2, 1])
 
-    def stores(i):
+    def stores(half):
+        some = pl.ds(half * (NX // 2), NX // 2)
         return (
-            pltpu.make_async_copy(out.at[0:3, i], vout.at[:, i], store_sem.at[0, i]),
-            pltpu.make_async_copy(out.at[3, i], pout.at[i], store_sem.at[1, i]),
+            pltpu.make_async_copy(out.at[0:3, some], vout.at[:, some], store_sem.at[0, half]),
+            pltpu.make_async_copy(out.at[3, some], pout.at[some], store_sem.at[1, half]),
         )
 
     def last(i, _):
@@ -591,15 +589,15 @@
             new = fine_update(u4, ends4, i, t)
             for k in range(4):
                 out[k, i, pl.ds(8 * t, 8), :] = new[k]
-        for store in stores(i):
+        return 0
+
+    for half in range(2):
+        lax.fori_loop(half * (NX // 2), (half + 1) * (NX // 2), last, 0, unroll=2)
+        for store in stores(half):
             store.start()
-        return 0
-
-    lax.fori_loop(0, NX, last, 0, unroll=2)
-    for i in range(NX):
-        for store in stores(i):
+    for half in range(2):
+        for store in stores(half):
             store.wait()
-    drain()
 
 
 def cycle(size, velocity, pressure, viscosity, body_force):
@@ -655,7 +653,7 @@
             pltpu.SemaphoreType.DMA((2, len(AROUND))),
             pltpu.SemaphoreType.DMA((2, len(AROUND))),
             pltpu.SemaphoreType.DMA((4,)),
-            pltpu.SemaphoreType.DMA((2, NX)),
+            pltpu.SemaphoreType.DMA((2, 2)),
         ],
         compiler_params=pltpu.CompilerParams(collective_id=0, has_side_effects=True),
         name="cycle",

time: 34.6 us -> 33.8 us (0.977)
  Pallas kernels: 31.3 us -> 30.5 us
    pallas_call x1, Pallas kernels: 31.3 us -> 30.5 us  [cycle(): pl.pallas_call(functools.partial(kernel, size), out_shape=(jax.ShapeDtype...]
where the time goes in v4:
time: 33.8 us; the launch traced here: 33.6 us
  Pallas kernels  30.5 us (90%)
  local copies, waits for them, and re-layouts  2.46 us (7%)
  between operations  0.65 us (2%)
    pallas_call x1, Pallas kernels, cycle(): pl.pallas_call(functools.partial(kernel, size), out_shape=(jax.ShapeDtype...  30.5 us
    unnamed x4, local copies, waits for them, and re-layouts  2.46 us

profile of v4, /device:TPU:1, one launch (start us, length us, event | category | flops | bytes accessed | tf_op | source)
XLA Modules:
  0.0 33.6 jit_solution(4147864646390651454)
XLA Ops:
  0.6 30.5 %cycle.1 = (f32[3,8,32,128]{3,2,1,0:T(8,128)}, f32[8,32,128]{2,1,0:T(8,128)}) custom-call(f32[3,8,32,128]{3,2,1,0:T(8,128)} %vel.1, f32[8,32,128]{2,1,0:T(8,128)} %prs.1, f32[8,32,128]{2,1,0:T(8,128)} %vis.1, f32[3,8,32,128]{3,2,1,0:T(8,128)} %frc.1), custom_call_target="tpu_custom_call" | custom-call | tf_op jit(solution)/shard_map/cycle/pallas_call | solution.py:618
  31.2 0.0 copy-start
  31.2 1.8 %copy.8 = f32[3,8,32,128]{3,2,1,0:T(8,128)} copy(f32[3,8,32,128]{3,2,1,0:T(8,128)} %get-tuple-element.4) | data formatting | bytes 786432
  33.0 0.0 copy-done
  33.0 0.7 %copy.9 = f32[8,32,128]{2,1,0:T(8,128)} copy(f32[8,32,128]{2,1,0:T(8,128)S(1)} %copy-done) | data formatting | bytes 262144
Async XLA Ops:
  31.2 1.8 %copy-start = (f32[8,32,128]{2,1,0:T(8,128)S(1)}, f32[8,32,128]{2,1,0:T(8,128)}, u32[]{:S(2)}) copy-start(f32[8,32,128]{2,1,0:T(8,128)} %get-tuple-element.5) | copy-start | bytes 393220

commit v5 on v4

--- a/solution.py
+++ b/solution.py
@@ -27,10 +27,10 @@
 def kernel(
     size, vel, prs, vis, frc, vout, pout,
     u0, u1, u2, u3, u4, visc, force, hvisc, c1, c2, c3, c4,
-    wts, scl, diag, rhs, cwts, cscl, tmp, grown, gprev, gnext, yprev, ynext, out,
+    wts, scl, diag, rhs, cwts, cscl, tmp, grown, gprev, gnext, yprev, ynext,
     ysend0, yrecv0, ysend, yrecv,
     vx, vy, vxb, vzb, vyc, vyz, cx, cy, cxb, czb, cyc, cyz,
-    send_sem, recv_sem, deep_send, deep_recv, load_sem, store_sem,
+    send_sem, recv_sem, deep_send, deep_recv, load_sem,
 ):
     at = {axis: lax.axis_index(axis) for axis in AXES}
     has = {}
@@ -127,7 +127,7 @@
             each(1, lambda c: c.start(), hops)
 
         pending.append(lambda: each(1, lambda c: c.wait_send()))
-        return start, (lambda: each(-1, lambda c: c.wait_recv()))
+        return start, (lambda *hops: each(-1, lambda c: c.wait_recv(), hops))
 
     zs = pl.ds(TOP, NZ)
     planes = pl.ds(1, NX)
@@ -270,6 +270,25 @@
                         pack = jnp.where(first | last, roll(xs[f, pp, pl.ds(8 * t, 8), :], 8 * s), pack)
             ys[n] = pack
 
+    def lay_own(value, odd):
+        return roll(value, NY // 2) if odd else value
+
+    def near_unpack(h, xs, ys, xb, zb, yc, yz):
+        sides = jnp.where(fore, yc[1, 1, 0], yc[1, 0, 0])
+        for i in range(CX):
+            pp, odd = i // 2, i % 2
+            for t in range(2):
+                own = lay_own(xs[0, pp, pl.ds(8 * t, 8), :], odd)
+                ends_here = roll(sides, NY // 2 - 8 * (deep_slot(0, pp, t) + 8 * odd))
+                h[0, CX + i, pl.ds(OWN + 8 * t, 8), :] = jnp.where(first_half, own, ends_here)
+            both = lay_own(zb[1, 0, pp], odd)
+            h[0, CX + i, pl.ds(TOP, DEEP), :] = both[0:DEEP]
+            h[0, CX + i, pl.ds(OWN + CZ, DEEP), :] = both[DEEP : 2 * DEEP]
+        for t in range(2):
+            rows = pl.ds(8 * t, 8)
+            h[0, CX - 1, pl.ds(OWN + 8 * t, 8), :] = lay_own(xb[0, 0, 1, rows, :], 1)
+            h[0, 2 * CX, pl.ds(OWN + 8 * t, 8), :] = lay_own(xb[1, 0, 0, rows, :], 0)
+
     def deep_unpack(h, nf, xs, ys, xb, zb, yc, yz):
         for dx in range(3):
             middle, corner = [], []
@@ -280,8 +299,7 @@
             block = xs if dx == 1 else xb.at[0 if dx == 0 else 1]
 
             def lay(value, odd, s, sides):
-                own = roll(value, NY // 2) if odd else value
-                return jnp.where(first_half, own, roll(sides, NY // 2 - 8 * (s + 8 * odd)))
+                return jnp.where(first_half, lay_own(value, odd), roll(sides, NY // 2 - 8 * (s + 8 * odd)))
 
             for f in range(nf):
                 for i in range(CX):
@@ -439,9 +457,9 @@
     ends1 = joined_ends(yrecv.at[0, 0], yrecv.at[0, 1])
     wait = exchange(u2, lambda i, t: fine_update(u1, ends1, i, t), ysend.at[1], yrecv.at[1])
     rotate(u2)
-    visc_wait()
-    deep_unpack(hvisc, 1, *visc_refs)
-    lax.fori_loop(1, HX - 1, coarse_weights, 0, unroll=2)
+    visc_wait(1)
+    near_unpack(hvisc, *visc_refs)
+    lax.fori_loop(CX, 2 * CX, coarse_weights, 0, unroll=2)
 
     def flat(ref, pp, t):
         rows = pl.ds(DEEP + 8 * t, 8)
@@ -486,8 +504,11 @@
         return 0
 
     lax.fori_loop(0, NX, insert_ends, 0, unroll=2)
+    visc_wait(2, 3)
+    deep_unpack(hvisc, 1, *visc_refs)
+    lax.fori_loop(1, HX - 1, coarse_weights, 0, unroll=2)
     drain(1)
-    flow_wait()
+    flow_wait(1, 2, 3)
     deep_unpack(c1, 4, *flow_refs)
 
     def coarse_sweep(old, new, start, stop):
@@ -577,27 +598,17 @@
     wait()
     ends4 = joined_ends(yrecv.at[2, 0], yrecv.at[2, 1])
 
-    def stores(half):
-        some = pl.ds(half * (NX // 2), NX // 2)
-        return (
-            pltpu.make_async_copy(out.at[0:3, some], vout.at[:, some], store_sem.at[0, half]),
-            pltpu.make_async_copy(out.at[3, some], pout.at[some], store_sem.at[1, half]),
-        )
-
     def last(i, _):
         for t in range(4):
             new = fine_update(u4, ends4, i, t)
             for k in range(4):
-                out[k, i, pl.ds(8 * t, 8), :] = new[k]
-        return 0
-
-    for half in range(2):
-        lax.fori_loop(half * (NX // 2), (half + 1) * (NX // 2), last, 0, unroll=2)
-        for store in stores(half):
-            store.start()
-    for half in range(2):
-        for store in stores(half):
-            store.wait()
+                if k < 3:
+                    vout[k, i, pl.ds(8 * t, 8), :] = new[k]
+                else:
+                    pout[i, pl.ds(8 * t, 8), :] = new[k]
+        return 0
+
+    lax.fori_loop(0, NX, last, 0, unroll=2)
 
 
 def cycle(size, velocity, pressure, viscosity, body_force):
@@ -622,7 +633,7 @@
             jax.ShapeDtypeStruct((NX, NZ, NY), F32),
         ),
         in_specs=[anywhere] * 4,
-        out_specs=(anywhere, anywhere),
+        out_specs=(pl.BlockSpec(memory_space=pltpu.VMEM),) * 2,
         scratch_shapes=[
             field, field, field, field, field,
             pltpu.VMEM((NX + 2, NZ + 16, NY), F32),
@@ -641,7 +652,6 @@
             pltpu.VMEM((4, CX, NZ, NY), F32),
             pltpu.VMEM((5, NX, NZ, NY), F32),
             pltpu.VMEM((5, NX, NZ, NY), F32),
-            pltpu.VMEM((4, NX, NZ, NY), F32),
             pltpu.VMEM((3, 8, NY), F32),
             pltpu.VMEM((2, 3, 8, NY), F32),
             pltpu.VMEM((3, 2, 8, NY), F32),
@@ -653,11 +663,10 @@
             pltpu.SemaphoreType.DMA((2, len(AROUND))),
             pltpu.SemaphoreType.DMA((2, len(AROUND))),
             pltpu.SemaphoreType.DMA((4,)),
-            pltpu.SemaphoreType.DMA((2, 2)),
         ],
-        compiler_params=pltpu.CompilerParams(collective_id=0, has_side_effects=True),
+        compiler_params=pltpu.CompilerParams(collective_id=0, has_side_effects=True, vmem_limit_bytes=25165824),
         name="cycle",
-    )(velocity, pressure, viscosity, body_force)
+    )(*[pltpu.with_memory_space_constraint(x, pltpu.HBM) for x in (velocity, pressure, viscosity, body_force)])
     return out[0], out[1]
 
 

time: 33.8 us -> 31.9 us (0.944)
  local copies, waits for them, and re-layouts: 2.46 us -> 1.4 us
  Pallas kernels: 30.5 us -> 29.7 us
    unnamed x4 -> x2, local copies, waits for them, and re-layouts: 2.46 us -> 1.4 us
    pallas_call x1, Pallas kernels: 30.5 us -> 29.7 us  [cycle(): pl.pallas_call(functools.partial(kernel, size), out_shape=(jax.ShapeDtype...]
where the time goes in v5:
time: 31.9 us; the launch traced here: 31.7 us
  Pallas kernels  29.7 us (93%)
  local copies, waits for them, and re-layouts  1.4 us (4%)
  between operations  0.64 us (2%)
    pallas_call x1, Pallas kernels, cycle(): pl.pallas_call(functools.partial(kernel, size), out_shape=(jax.ShapeDtype...  29.7 us
    unnamed x2, local copies, waits for them, and re-layouts  1.4 us

profile of v5, /device:TPU:1, one launch (start us, length us, event | category | flops | bytes accessed | tf_op | source)
XLA Modules:
  0.0 31.7 jit_solution(5969890572277711665)
XLA Ops:
  0.6 29.7 %cycle.1 = (f32[3,8,32,128]{3,2,1,0:T(8,128)S(1)}, f32[8,32,128]{2,1,0:T(8,128)S(1)}) custom-call(f32[3,8,32,128]{3,2,1,0:T(8,128)} %vel.1, f32[8,32,128]{2,1,0:T(8,128)} %prs.1, f32[8,32,128]{2,1,0:T(8,128)} %vis.1, f32[3,8,32,128]{3,2,1,0:T(8,128)} %frc.1), custom_call_target="tpu_custom_call" | custom-call | tf_op jit(solution)/shard_map/cycle/pallas_call | solution.py:629
  30.3 0.7 %copy.8 = f32[3,8,32,128]{3,2,1,0:T(8,128)} copy(f32[3,8,32,128]{3,2,1,0:T(8,128)S(1)} %get-tuple-element.4) | data formatting | bytes 786432
  31.1 0.7 %copy.9 = f32[8,32,128]{2,1,0:T(8,128)} copy(f32[8,32,128]{2,1,0:T(8,128)S(1)} %get-tuple-element.5) | data formatting | bytes 262144

commit v6 on v5

--- a/solution.py
+++ b/solution.py
@@ -223,7 +223,7 @@
             c = put(c, visc[i + 1, rows, :], slot_of(0, i, t))
         return a, b, c
 
-    packs = lax.fori_loop(0, NX, first_pack, (nil, nil, nil), unroll=2)
+    packs = lax.fori_loop(0, NX, first_pack, (nil, nil, nil), unroll=True)
     for n in range(3):
         ysend0[n] = packs[n]
 
@@ -361,7 +361,7 @@
                 rhs[k, i, rows, :] = (2.0 * scale) * force[k, i, rows, :]
         return 0
 
-    lax.fori_loop(0, NX, weights, 0, unroll=2)
+    lax.fori_loop(0, NX, weights, 0, unroll=True)
 
     def coarse_weights(x, _):
         for t in range(3):
@@ -432,7 +432,7 @@
         packs = plane(NX - 1, plane(0, (nil, nil)))
         x_start, x_wait = x_pair(u)
         x_start()
-        packs = lax.fori_loop(1, NX - 1, plane, packs, unroll=2)
+        packs = lax.fori_loop(1, NX - 1, plane, packs, unroll=3)
         sent[0], sent[1] = packs
         z_start, z_wait = z_pair(u)
         z_start()
@@ -484,7 +484,7 @@
                 tmp[k, i, pl.ds(8 * t, 8), :] = sums[k]
         return 0
 
-    lax.fori_loop(0, CX, restrict, 0)
+    lax.fori_loop(0, CX, restrict, 0, unroll=True)
     for k in range(4):
         for pp in range(2):
             for t in range(2):
@@ -535,7 +535,7 @@
                 )
             return 0
 
-        lax.fori_loop(start, stop, plane, 0, unroll=2)
+        lax.fori_loop(start, stop, plane, 0, unroll=True)
 
     coarse_sweep(c1, c2, 1, HX - 1)
     coarse_sweep(c2, c3, 2, HX - 2)
@@ -566,8 +566,8 @@
                 widen(gnext.at[k, x - 1], 16 * t, pick(value, parents[2]))
         return 0
 
-    lax.fori_loop(0, CX + 2, prolong, 0, unroll=2)
-    lax.fori_loop(1, CX + 1, prolong_sides, 0, unroll=2)
+    lax.fori_loop(0, CX + 2, prolong, 0, unroll=True)
+    lax.fori_loop(1, CX + 1, prolong_sides, 0, unroll=True)
 
     def correct(i, _):
         half = lax.div(i + 1, 2)
@@ -579,7 +579,7 @@
                 u3[k, i, r : r + 1, :] = u2[k, i, r : r + 1, :] + grown[k, half, r : r + 1, :]
         return 0
 
-    lax.fori_loop(1, NX + 1, correct, 0, unroll=2)
+    lax.fori_loop(1, NX + 1, correct, 0, unroll=True)
     for i, x in ((0, 0), (NX + 1, CX + 1)):
         for k in range(4):
             for t in range(4):
@@ -608,7 +608,7 @@
                     pout[i, pl.ds(8 * t, 8), :] = new[k]
         return 0
 
-    lax.fori_loop(0, NX, last, 0, unroll=2)
+    lax.fori_loop(0, NX, last, 0, unroll=True)
 
 
 def cycle(size, velocity, pressure, viscosity, body_force):

time: 31.9 us -> 29.2 us (0.915)
  Pallas kernels: 29.7 us -> 27 us
    pallas_call x1, Pallas kernels: 29.7 us -> 27 us  [cycle(): pl.pallas_call(functools.partial(kernel, size), out_shape=(jax.ShapeDtype...]
where the time goes in v6:
time: 29.2 us; the launch traced here: 29.1 us
  Pallas kernels  27 us (92%)
  local copies, waits for them, and re-layouts  1.4 us (5%)
  between operations  0.64 us (2%)
    pallas_call x1, Pallas kernels, cycle(): pl.pallas_call(functools.partial(kernel, size), out_shape=(jax.ShapeDtype...  27 us
    unnamed x2, local copies, waits for them, and re-layouts  1.4 us

profile of v6, /device:TPU:1, one launch (start us, length us, event | category | flops | bytes accessed | tf_op | source)
XLA Modules:
  0.0 29.1 jit_solution(14310636493365831911)
XLA Ops:
  0.6 27.0 %cycle.1 = (f32[3,8,32,128]{3,2,1,0:T(8,128)S(1)}, f32[8,32,128]{2,1,0:T(8,128)S(1)}) custom-call(f32[3,8,32,128]{3,2,1,0:T(8,128)} %vel.1, f32[8,32,128]{2,1,0:T(8,128)} %prs.1, f32[8,32,128]{2,1,0:T(8,128)} %vis.1, f32[3,8,32,128]{3,2,1,0:T(8,128)} %frc.1), custom_call_target="tpu_custom_call" | custom-call | tf_op jit(solution)/shard_map/cycle/pallas_call | solution.py:629
  27.7 0.7 %copy.8 = f32[3,8,32,128]{3,2,1,0:T(8,128)} copy(f32[3,8,32,128]{3,2,1,0:T(8,128)S(1)} %get-tuple-element.4) | data formatting | bytes 786432
  28.4 0.7 %copy.9 = f32[8,32,128]{2,1,0:T(8,128)} copy(f32[8,32,128]{2,1,0:T(8,128)S(1)} %get-tuple-element.5) | data formatting | bytes 262144

commit v7 on v6

--- a/solution.py
+++ b/solution.py
@@ -21,7 +21,7 @@
     (d for d in itertools.product((-1, 0, 1), repeat=3) if any(d)),
     key=lambda d: (d[1:] != (0, 0), -sum(map(abs, d))),
 )
-FACES = 2 * (2 + 2 + 1 + 3 * 3)
+FACES = 2 * (2 + 2 + 1 + 3)
 
 
 def kernel(
@@ -112,7 +112,7 @@
             src, dst = deep_parts(d, *refs)
             return pltpu.make_async_remote_copy(
                 src_ref=src, dst_ref=dst,
-                send_sem=deep_send.at[which, k], recv_sem=deep_recv.at[which, k],
+                send_sem=deep_send.at[k], recv_sem=deep_recv.at[which, k],
                 device_id={axis: beside(axis, s) for axis, s in zip(AXES, d) if s}, device_id_type=MESH,
             )
 
@@ -289,13 +289,16 @@
             h[0, CX - 1, pl.ds(OWN + 8 * t, 8), :] = lay_own(xb[0, 0, 1, rows, :], 1)
             h[0, 2 * CX, pl.ds(OWN + 8 * t, 8), :] = lay_own(xb[1, 0, 0, rows, :], 0)
 
-    def deep_unpack(h, nf, xs, ys, xb, zb, yc, yz):
+    def deep_unpack(h, nf, hops, xs, ys, xb, zb, yc, yz):
         for dx in range(3):
+            far = 1 if dx == 1 else 2
             middle, corner = [], []
             for n in range((nf + 1) // 2):
-                middle.append(jnp.where(fore, yc[dx, 1, n], yc[dx, 0, n]))
-                value = jnp.where(fore, yz[dx, 1, n], yz[dx, 0, n])
-                corner.append(jnp.where(row < DEEP, roll(value, -4 * DEEP), value))
+                if far in hops:
+                    middle.append(jnp.where(fore, yc[dx, 1, n], yc[dx, 0, n]))
+                if far + 1 in hops:
+                    value = jnp.where(fore, yz[dx, 1, n], yz[dx, 0, n])
+                    corner.append(jnp.where(row < DEEP, roll(value, -4 * DEEP), value))
             block = xs if dx == 1 else xb.at[0 if dx == 0 else 1]
 
             def lay(value, odd, s, sides):
@@ -304,13 +307,15 @@
             for f in range(nf):
                 for i in range(CX):
                     pp, odd, x = i // 2, i % 2, dx * CX + i
-                    for t in range(2):
-                        h[f, x, pl.ds(OWN + 8 * t, 8), :] = lay(
-                            block[f, pp, pl.ds(8 * t, 8), :], odd, deep_slot(f, pp, t), middle[f // 2]
-                        )
-                    both = lay(zb[dx, f, pp], odd, deep_slot(f, pp, 0), corner[f // 2])
-                    h[f, x, pl.ds(TOP, DEEP), :] = both[0:DEEP]
-                    h[f, x, pl.ds(OWN + CZ, DEEP), :] = both[DEEP : 2 * DEEP]
+                    if far in hops:
+                        for t in range(2):
+                            h[f, x, pl.ds(OWN + 8 * t, 8), :] = lay(
+                                block[f, pp, pl.ds(8 * t, 8), :], odd, deep_slot(f, pp, t), middle[f // 2]
+                            )
+                    if far + 1 in hops:
+                        both = lay(zb[dx, f, pp], odd, deep_slot(f, pp, 0), corner[f // 2])
+                        h[f, x, pl.ds(TOP, DEEP), :] = both[0:DEEP]
+                        h[f, x, pl.ds(OWN + CZ, DEEP), :] = both[DEEP : 2 * DEEP]
 
     def average(i, _):
         for t in range(4):
@@ -455,8 +460,10 @@
     wait()
     visc_start(3)
     ends1 = joined_ends(yrecv.at[0, 0], yrecv.at[0, 1])
+    count[0] = 0
     wait = exchange(u2, lambda i, t: fine_update(u1, ends1, i, t), ysend.at[1], yrecv.at[1])
     rotate(u2)
+    drain(3)
     visc_wait(1)
     near_unpack(hvisc, *visc_refs)
     lax.fori_loop(CX, 2 * CX, coarse_weights, 0, unroll=2)
@@ -505,11 +512,12 @@
 
     lax.fori_loop(0, NX, insert_ends, 0, unroll=2)
     visc_wait(2, 3)
-    deep_unpack(hvisc, 1, *visc_refs)
+    deep_unpack(hvisc, 1, (1, 2, 3), *visc_refs)
     lax.fori_loop(1, HX - 1, coarse_weights, 0, unroll=2)
     drain(1)
-    flow_wait(1, 2, 3)
-    deep_unpack(c1, 4, *flow_refs)
+    for hops in (1, 2, 3):
+        flow_wait(hops)
+        deep_unpack(c1, 4, (hops,), *flow_refs)
 
     def coarse_sweep(old, new, start, stop):
         def plane(x, _):
@@ -592,6 +600,7 @@
         return yprev[k, i, rows, :] + gprev[k, half, rows, :], ynext[k, i, rows, :] + gnext[k, half, rows, :]
 
 
+    count[0] = FACES - 6
     wait = exchange(u4, lambda i, t: fine_update(u3, ends3, i, t), ysend.at[2], yrecv.at[2])
     rotate(u4)
     drain()
@@ -660,7 +669,7 @@
             *deep_buffers(4),
             pltpu.SemaphoreType.DMA((FACES,)),
             pltpu.SemaphoreType.DMA((FACES,)),
-            pltpu.SemaphoreType.DMA((2, len(AROUND))),
+            pltpu.SemaphoreType.DMA((len(AROUND),)),
             pltpu.SemaphoreType.DMA((2, len(AROUND))),
             pltpu.SemaphoreType.DMA((4,)),
         ],

time: 29.2 us -> 28.8 us (0.986)
  Pallas kernels: 27 us -> 26.6 us
    pallas_call x1, Pallas kernels: 27 us -> 26.6 us  [cycle(): pl.pallas_call(functools.partial(kernel, size), out_shape=(jax.ShapeDtype...]
where the time goes in v7:
time: 28.8 us; the launch traced here: 28.6 us
  Pallas kernels  26.6 us (92%)
  local copies, waits for them, and re-layouts  1.4 us (5%)
  between operations  0.64 us (2%)
    pallas_call x1, Pallas kernels, cycle(): pl.pallas_call(functools.partial(kernel, size), out_shape=(jax.ShapeDtype...  26.6 us
    unnamed x2, local copies, waits for them, and re-layouts  1.4 us

profile of v7, /device:TPU:1, one launch (start us, length us, event | category | flops | bytes accessed | tf_op | source)
XLA Modules:
  0.0 28.6 jit_solution(6751682339958583572)
XLA Ops:
  0.6 26.6 %cycle.1 = (f32[3,8,32,128]{3,2,1,0:T(8,128)S(1)}, f32[8,32,128]{2,1,0:T(8,128)S(1)}) custom-call(f32[3,8,32,128]{3,2,1,0:T(8,128)} %vel.1, f32[8,32,128]{2,1,0:T(8,128)} %prs.1, f32[8,32,128]{2,1,0:T(8,128)} %vis.1, f32[3,8,32,128]{3,2,1,0:T(8,128)} %frc.1), custom_call_target="tpu_custom_call" | custom-call | tf_op jit(solution)/shard_map/cycle/pallas_call | solution.py:638
  27.2 0.7 %copy.8 = f32[3,8,32,128]{3,2,1,0:T(8,128)} copy(f32[3,8,32,128]{3,2,1,0:T(8,128)S(1)} %get-tuple-element.4) | data formatting | bytes 786432
  28.0 0.7 %copy.9 = f32[8,32,128]{2,1,0:T(8,128)} copy(f32[8,32,128]{2,1,0:T(8,128)S(1)} %get-tuple-element.5) | data formatting | bytes 262144
